TPU v7x, 32 devices: a whole 2x2x4 slice. The times are simulated.
32 devices in a mesh: tile: 4 (over z), text: 8 (over y, x, core).
Axes of the slice: x: 2, y: 2, z: 4, core: 2. Of those that a mesh axis runs over, the one named last changes fastest.
Arguments:
- grad_seq: bfloat16 [2560, 8192], P('text', 'tile'), may hold values from -6 to 6
- positions: int32 [2560], replicated, may hold values from 0 to 2559, each once
- pre_act: bfloat16 [2560, 5120], P('tile', 'text'), may hold values from -6 to 6
- w_out: bfloat16 [5120, 8192], P('text', 'tile'), may hold values from -0.078125 to 0.078125
Outputs:
- grad_pre: float32 [2560, 5120], P('tile', 'text')
- grad_w_out: float32 [5120, 8192], P('text', 'tile')
- grad_bias: float32 [8192], P('tile')
Inputs may be any that keep to these rules, and one draw needn't show every extreme that they name: positions names every place 0 to 2559 once.
All inputs are finite; a program needn't handle non-finite values.
Results may differ from a plain program's by a relative error of at most 0.003.
Values may be sent and summed in bfloat16 or wider, within the bound.
A program may use at most 128 MiB of HBM per device.

v0:
```python
import jax
import jax.numpy as jnp
from jax import lax
from jax.sharding import PartitionSpec as P


def gelu_parts(pre):
    value = pre.astype(jnp.float32)
    cdf = 0.5 * (1.0 + jax.scipy.special.erf(value * 0.7071067811865476))
    activated = value * cdf
    slope = cdf + value * jnp.exp(-0.5 * value * value) * 0.3989422804014327
    return (activated, slope)


def body(grad_seq, positions, pre_act, w_out):
    local_rows = pre_act.shape[0]
    pre_all = lax.all_gather(pre_act, "tile", axis=0, tiled=True)
    activated, slope_all = gelu_parts(pre_all)
    act_bf = activated.astype(jnp.bfloat16)
    slope = lax.dynamic_slice_in_dim(slope_all, lax.axis_index("tile") * local_rows, local_rows, 0)
    gathered = lax.all_gather(grad_seq, "text", axis=0, tiled=True)
    slot_grad = jnp.take(gathered, positions, axis=0)
    grad_act = jnp.einsum("so,ho->sh", slot_grad, w_out, preferred_element_type=jnp.float32)
    weight_term = jnp.einsum("sh,so->ho", act_bf, slot_grad, preferred_element_type=jnp.float32)
    local_sum = jnp.sum(gathered, axis=0, dtype=jnp.float32)
    summed_act = lax.psum_scatter(grad_act, "tile", scatter_dimension=0, tiled=True)
    grad_pre = summed_act * slope
    return (grad_pre, weight_term, local_sum)


def solution(mesh):
    in_specs = (P("text", "tile"), P(), P("tile", "text"), P("text", "tile"))
    out_specs = (P("tile", "text"), P("text", "tile"), P("tile"))
    return jax.shard_map(body, mesh=mesh, in_specs=in_specs, out_specs=out_specs, check_vma=False)
```

profile of v0, /device:TPU:0, one launch (start us, length us, event | category | flops | bytes accessed | tf_op | source)
XLA Modules:
  0.0 269.5 jit_solution(6813738380469028711)
XLA Ops:
  7.2 0.0 copy-start
  7.2 0.0 all-gather.3.cloned.1.call-start
  7.2 0.7 all-gather.3.cloned.1.call-update
  7.9 0.0 all-gather.5.cloned.1.call-start
  8.0 0.7 all-gather.5.cloned.1.call-update
  8.7 0.0 reduce-scatter.2.cloned.1.call-start
  8.7 0.7 compare_select_fusion
  9.4 0.7 compare_and_fusion
  10.2 65.6 %all-gather.3.cloned.1.call-done = bf16[2560,2048]{1,0:T(8,128)(2,1)} async-done(((bf16[320,2048]{1,0:T(8,128)(2,1)}), bf16[2560,2048]{1,0:T(8,128)(2,1)}) %all-gather.3.cloned.1.call-update) | async-done | bytes 10485776 | tf_op jit(solution)/shard_map/all_gather | solution.py:21
  75.8 25.5 %gather_fusion = bf16[2560,2048]{1,0:T(8,128)(2,1)} fusion(bf16[2560,2048]{1,0:T(8,128)(2,1)} %all-gather.3.cloned.1.call-done, s32[3072]{0:T(1024)S(1)} %pad_clamp_fusion), kind=kCustom, calls=%fused_computation | custom fusion | bytes 20981760 | tf_op jit(solution)/shard_map/jit(_take)/gather | solution.py:22
  101.3 0.0 copy-done
  101.3 13.5 %fusion.1 = f32[2560,640]{1,0:T(8,128)} fusion(bf16[640,2048]{1,0:T(8,128)(2,1)S(1)} %copy-done, bf16[2560,2048]{1,0:T(8,128)(2,1)} %gather_fusion, pred[2560]{0:T(1024)(128)(4,1)S(1)} %compare_and_fusion), kind=kOutput, calls=%fused_computation.6 | convolution fusion | flops 6716129280 | bytes 19663360 | tf_op jit(solution)/shard_map/so,ho->sh/dot_general | solution.py:23
  114.7 0.0 reduce-scatter.2.cloned.1.call-update
  114.8 28.2 %all-gather.5.cloned.1.call-done = bf16[2560,640]{1,0:T(8,128)(2,1)} async-done(((bf16[640,640]{1,0:T(8,128)(2,1)}), bf16[2560,640]{1,0:T(8,128)(2,1)}) %all-gather.5.cloned.1.call-update) | async-done | bytes 3276816 | tf_op jit(solution)/shard_map/all_gather | solution.py:17
  143.0 0.0 slice-start
  143.0 0.0 slice-start.1
  143.0 5.8 %convert_element_type.9 = f32[2560,640]{1,0:T(8,128)} convert(bf16[2560,640]{1,0:T(8,128)(2,1)} %all-gather.5.cloned.1.call-done) | non-fusion elementwise | flops 1638400 | bytes 9830400 | tf_op jit(solution)/shard_map/convert_element_type | solution.py:8
  148.8 0.0 slice-start.2
  148.8 5.3 %add_multiply_fusion = f32[2560,640]{1,0:T(8,128)} fusion(bf16[2560,640]{1,0:T(8,128)(2,1)} %all-gather.5.cloned.1.call-done), kind=kLoop, calls=%fused_computation.4 | loop fusion | flops 6553600 | bytes 9830400 | tf_op jit(solution)/shard_map/mul | solution.py:9
  154.0 0.0 slice-done
  154.0 0.0 slice-done.1
  154.0 0.0 slice-done.2
  154.0 2.2 convert_reduce_fusion
  156.3 14.2 %fusion = f32[640,2048]{1,0:T(8,128)} fusion(bf16[2560,2048]{1,0:T(8,128)(2,1)} %gather_fusion, pred[2560]{0:T(1024)(128)(4,1)S(1)} %compare_and_fusion, f32[2560,640]{1,0:T(8,128)} %add_multiply_fusion, bf16[2560,640]{1,0:T(8,128)(2,1)} %all-gather.5.cloned.1.call-done), kind=kOutput, calls=%fused_computation.5 | convolution fusion | flops 6721044480 | bytes 25561600 | tf_op jit(solution)/shard_map/sh,so->ho/dot_general | solution.py:24
  170.4 88.5 %reduce-scatter.2.cloned.1.call-done = f32[640,640]{1,0:T(8,128)} async-done(((f32[2560,640]{1,0:T(8,128)}), f32[640,640]{1,0:T(8,128)}) %reduce-scatter.2.cloned.1.call-update) | async-done | bytes 1638416 | tf_op jit(solution)/shard_map/reduce_scatter | solution.py:26
  258.9 4.0 %fusion.7 = f32[640,640]{1,0:T(8,128)} fusion(f32[640,640]{1,0:T(8,128)} %reduce-scatter.2.cloned.1.call-done, f32[2560,640]{1,0:T(8,128)} %add_multiply_fusion, s32[]{:T(128)S(6)} %select_n.14, f32[2560,640]{1,0:T(8,128)} %convert_element_type.9), kind=kLoop, calls=%fused_computation.13 | loop fusion | flops 2457600 | bytes 6553604 | tf_op jit(solution)/shard_map/mul | solution.py:27
  (2 shorter events, 0.0 us)
Async XLA Ops:
  7.2 94.1 %copy-start = (bf16[640,2048]{1,0:T(8,128)(2,1)S(1)}, bf16[640,2048]{1,0:T(8,128)(2,1)}, u32[]{:S(2)}) copy-start(bf16[640,2048]{1,0:T(8,128)(2,1)} %param.7) | copy-start | bytes 7864324
  7.2 68.6 %all-gather.3.cloned.1.call-start = ((), (), s32[]{:S(2)}) async-start(), calls=%async_computation.1 | async-start | bytes 11796480 | tf_op jit(solution)/shard_map/all_gather | solution.py:21
  7.9 135.0 %all-gather.5.cloned.1.call-start = ((), (), s32[]{:S(2)}) async-start(), calls=%async_computation.3 | async-start | bytes 4096000 | tf_op jit(solution)/shard_map/all_gather | solution.py:17
  8.7 250.3 %reduce-scatter.2.cloned.1.call-start = ((), (), s32[]{:S(2)}) async-start(), calls=%async_computation.2 | async-start | bytes 8192000 | tf_op jit(solution)/shard_map/reduce_scatter | solution.py:26
  143.0 11.1 %slice-start = ((s8[10485760]{0:T(1024)(128)(4,1)}), s8[4194304]{0:T(1024)(128)(4,1)S(1)}, s32[]{:S(2)}) async-start(s8[10485760]{0:T(1024)(128)(4,1)} %bitcast.1), calls=%async_computation.4 | async-start | bytes 8388608
  143.0 11.1 %slice-start.1 = ((s8[10485760]{0:T(1024)(128)(4,1)}), s8[4194304]{0:T(1024)(128)(4,1)S(1)}, s32[]{:S(2)}) async-start(s8[10485760]{0:T(1024)(128)(4,1)} %bitcast.1), calls=%async_computation.5 | async-start | bytes 8388608
  148.8 5.3 %slice-start.2 = ((s8[10485760]{0:T(1024)(128)(4,1)}), s8[2097152]{0:T(1024)(128)(4,1)S(1)}, s32[]{:S(2)}) async-start(s8[10485760]{0:T(1024)(128)(4,1)} %bitcast.1), calls=%async_computation.6 | async-start | bytes 4194304
Sparse Core Ops, SparseCore 0:
  9.9 65.8 all-gather.2
  77.3 65.5 all-gather.4
  145.3 113.6 reduce-scatter.1
where the time goes:
time: 270 us; the launch traced here: 269 us
  waiting for transfers between devices  184 us (68%)
  matrix products  27.7 us (10%)
  local copies, waits for them, and re-layouts  25.5 us (9%)
  other arithmetic  18.7 us (7%)
  between operations  13.8 us (5%)
    reduce_scatter x1, waiting for transfers between devices, body(): lax.psum_scatter(grad_act, 'tile', scatter_dimension=0, tiled=True)  88.5 us
    all_gather x1, waiting for transfers between devices, body(): gathered = lax.all_gather(grad_seq, 'text', axis=0, tiled=True)  65.6 us
    all_gather x1, waiting for transfers between devices, body(): pre_all = lax.all_gather(pre_act, 'tile', axis=0, tiled=True)  28.2 us
    gather x1, local copies, waits for them, and re-layouts, body(): slot_grad = jnp.take(gathered, positions, axis=0)  25.5 us
    dot_general x1, matrix products, body(): jnp.einsum('sh,so->ho', act_bf, slot_grad, preferred_element_type=jnp.flo...  14.2 us
    dot_general x1, matrix products, body(): jnp.einsum('so,ho->sh', slot_grad, w_out, preferred_element_type=jnp.floa...  13.5 us
    convert_element_type x1, other arithmetic, gelu_parts(): value = pre.astype(jnp.float32)  5.8 us
  transfers between devices with their start and end apart: 3, of which 3 were waited for; matrix products, arithmetic and copies ran while one was open for 25% of the time, Pallas kernels for 0%

commit v1 on v0

v1 whole, which is shorter than its diff:
```python
import jax
import jax.numpy as jnp
from jax import lax
from jax.sharding import PartitionSpec as P


def gelu_parts(pre):
    value = pre.astype(jnp.float32)
    cdf = 0.5 * (1.0 + jax.scipy.special.erf(value * 0.7071067811865476))
    activated = value * cdf
    slope = cdf + value * jnp.exp(-0.5 * value * value) * 0.3989422804014327
    return (activated, slope)


def rows_of(table, index):
    return table.at[index].get(mode="promise_in_bounds", unique_indices=True)


def line_sum(term, me, n, rows):
    def mine(block):
        start = jnp.clip(block, 0, n - 1) * rows
        return lax.dynamic_slice_in_dim(term, start, rows, 0).astype(jnp.float32)

    total = mine(me)
    right = left = None
    for step in range(1, n):
        ahead = n - step
        out_right, out_left = mine(me + ahead), mine(me - ahead)
        if right is not None:
            out_right = out_right + right.astype(jnp.float32)
            out_left = out_left + left.astype(jnp.float32)
        hops = range(min(step, n - 1))
        right = lax.ppermute(out_right.astype(jnp.bfloat16), "tile", [(i, i + 1) for i in hops])
        left = lax.ppermute(out_left.astype(jnp.bfloat16), "tile", [(n - 1 - i, n - 2 - i) for i in hops])
    return total + right.astype(jnp.float32) + left.astype(jnp.float32)


def solution(mesh):
    n_tile = mesh.shape["tile"]

    def body(grad_seq, positions, pre_act, w_out):
        local_rows, hidden = pre_act.shape
        slots = positions.shape[0]
        me = lax.axis_index("tile")
        gathered = lax.all_gather(grad_seq, "text", axis=0, tiled=True)

        blocks = [pre_act]
        for shift in range(1, n_tile):
            ring = [(i, (i + shift) % n_tile) for i in range(n_tile)]
            blocks.append(lax.ppermute(pre_act, "tile", ring))
        slot = jnp.arange(slots, dtype=jnp.int32)
        turned = (me - slot // local_rows) % n_tile * local_rows + slot % local_rows
        source = jnp.zeros((slots,), jnp.int32).at[positions].set(
            turned, mode="promise_in_bounds", unique_indices=True)
        act = jnp.concatenate([gelu_parts(b)[0].astype(jnp.bfloat16) for b in blocks], axis=0)
        act_seq = rows_of(act, source)
        slope = gelu_parts(pre_act)[1]
        gathered, act_seq, slope = lax.optimization_barrier((gathered, act_seq, slope))

        cut = hidden // 2 // 128 * 128
        spans = [(0, cut), (cut, hidden)] if cut else [(0, hidden)]
        summed = []
        for lo, hi in spans:
            term = jnp.einsum("so,ho->sh", gathered, w_out[lo:hi], preferred_element_type=jnp.float32)
            term = rows_of(term.astype(jnp.bfloat16), positions)
            summed.append(line_sum(term, me, n_tile, local_rows))
        weight_term = jnp.einsum("sh,so->ho", act_seq, gathered, preferred_element_type=jnp.float32)
        local_sum = jnp.sum(gathered, axis=0, dtype=jnp.float32)
        grad_pre = jnp.concatenate(summed, axis=1) * slope
        return (grad_pre, weight_term, local_sum)

    in_specs = (P("text", "tile"), P(), P("tile", "text"), P("text", "tile"))
    out_specs = (P("tile", "text"), P("text", "tile"), P("tile"))
    return jax.shard_map(body, mesh=mesh, in_specs=in_specs, out_specs=out_specs, check_vma=False)
```

time: 270 us -> 216 us (0.80)
  waiting for transfers between devices: 184 us -> 73.8 us
  starting transfers between devices: 0.11 us -> 36.4 us
  local copies, waits for them, and re-layouts: 25.5 us -> 39.6 us
  other arithmetic: 18.7 us -> 26.5 us
    reduce_scatter x1 -> x0, waiting for transfers between devices: 88.5 us -> none  [body(): lax.psum_scatter(grad_act, 'tile', scatter_dimension=0, tiled=True)]
    ppermute x0 -> x15, waiting for transfers between devices: none -> 73.1 us  [the longest x3 55.8 us: body(): blocks.append(lax.ppermute(pre_act, 'tile', ring))]
    all_gather x1, waiting for transfers between devices: 65.6 us -> 0.01 us  [body(): gathered = lax.all_gather(grad_seq, 'text', axis=0, tiled=True)]
    ppermute x0 -> x15, starting transfers between devices: none -> 36.3 us  [the longest x6 23.3 us: line_sum(): lax.ppermute(out_right.astype(jnp.bfloat16), 'tile', [(i, i + 1) for i in...]
    all_gather x1 -> x0, waiting for transfers between devices: 28.2 us -> none  [body(): pre_all = lax.all_gather(pre_act, 'tile', axis=0, tiled=True)]
    scatter x0 -> x1, local copies, waits for them, and re-layouts: none -> 9.93 us  [body(): jnp.zeros((slots,), jnp.int32).at[positions]]
    mul x2 -> x1, other arithmetic: 9.27 us -> 1.33 us  [body(): grad_pre = jnp.concatenate(summed, axis=1) * slope]
    concatenate x0 -> x1, other arithmetic: none -> 7.56 us  [body(): jnp.concatenate([gelu_parts(b)[0].astype(jnp.bfloat16) for b in blocks],...]
  transfers between devices with their start and end apart: 3 -> 16, of which waited for: 3 -> 7; matrix products, arithmetic and copies ran while one was open for 25% -> 30% of each run, Pallas kernels for 0% -> 0%
where the time goes in v1:
time: 216 us
  waiting for transfers between devices  73.8 us (34%)
  local copies, waits for them, and re-layouts  39.6 us (18%)
  starting transfers between devices  36.4 us (17%)
  other arithmetic  26.5 us (12%)
  matrix products  25.3 us (12%)
  between operations  14.3 us (7%)
    ppermute x3, waiting for transfers between devices, body(): blocks.append(lax.ppermute(pre_act, 'tile', ring))  55.8 us
    gather x3, local copies, waits for them, and re-layouts, rows_of(): return table.at[index].get(mode='promise_in_bounds', unique_indices=True)  24.6 us
    ppermute x6, starting transfers between devices, line_sum(): lax.ppermute(out_right.astype(jnp.bfloat16), 'tile', [(i, i + 1) for i in...  23.3 us
    dot_general x2, matrix products, body(): jnp.einsum('so,ho->sh', gathered, w_out[lo:hi], preferred_element_type=jn...  13.2 us
    dot_general x1, matrix products, body(): jnp.einsum('sh,so->ho', act_seq, gathered, preferred_element_type=jnp.flo...  12.1 us
    ppermute x6, waiting for transfers between devices, line_sum(): lax.ppermute(out_right.astype(jnp.bfloat16), 'tile', [(i, i + 1) for i in...  11.2 us
    scatter x1, local copies, waits for them, and re-layouts, body(): jnp.zeros((slots,), jnp.int32).at[positions]  9.93 us
    concatenate x1, other arithmetic, body(): jnp.concatenate([gelu_parts(b)[0].astype(jnp.bfloat16) for b in blocks],...  7.56 us
  transfers between devices with their start and end apart: 16, of which 7 were waited for; matrix products, arithmetic and copies ran while one was open for 30% of the time, Pallas kernels for 0%

profile of v1, /device:TPU:0, one launch (start us, length us, event | category | flops | bytes accessed | tf_op | source)
XLA Modules:
  0.0 215.8 jit_solution(15609552473671607583)
XLA Ops:
  7.2 0.7 all-gather.2.cloned.1.call-update
  7.9 5.1 %collective-permute-start.2 = (bf16[640,640]{1,0:T(8,128)(2,1)}, bf16[640,640]{1,0:T(8,128)(2,1)S(1)}, u32[]{:S(2)}, u32[]{:S(2)}) collective-permute-start(bf16[640,640]{1,0:T(8,128)(2,1)} %param.6), channel_id=1, source_target_pairs={{0,24},{8,0},{16,8},{24,16},{1,25},{9,1},{17,9},{25,17},{2,26},{10... | collective-permute-start | bytes 2457608 | tf_op jit(solution)/shard_map/ppermute | solution.py:50
  13.0 1.0 collective-permute-start.1
  14.1 0.7 compare_select_fusion.1
  14.8 9.9 %scatter_custom_fusion = s32[2560]{0:T(1024)S(1)} fusion(s32[2560]{0:T(1024)S(1)} %get-tuple-element.19, s32[2560]{0:T(1024)S(1)} %get-tuple-element.20, s32[]{:T(128)} %constant.49.clone.1), kind=kCustom, calls=%fused_computation.73 | custom fusion | bytes 10244 | tf_op jit(solution)/shard_map/scatter | solution.py:53
  24.8 1.9 fusion.18
  26.7 5.3 %collective-permute-done.2 = bf16[640,640]{1,0:T(8,128)(2,1)S(1)} collective-permute-done((bf16[640,640]{1,0:T(8,128)(2,1)}, bf16[640,640]{1,0:T(8,128)(2,1)S(1)}, u32[]{:S(2)}, u32[]{:S(2)}) %collective-permute-start.2) | collective-permute-done | bytes 819232 | tf_op jit(solution)/shard_map/ppermute | solution.py:50
  32.0 0.4 fusion.11
  32.4 18.1 %collective-permute-done = bf16[640,640]{1,0:T(8,128)(2,1)S(1)} collective-permute-done((bf16[640,640]{1,0:T(8,128)(2,1)}, bf16[640,640]{1,0:T(8,128)(2,1)S(1)}, u32[]{:S(2)}, u32[]{:S(2)}) %collective-permute-start) | collective-permute-done | bytes 819232 | tf_op jit(solution)/shard_map/ppermute | solution.py:50
  50.4 0.4 fusion.3
  50.8 32.5 %collective-permute-done.1 = bf16[640,640]{1,0:T(8,128)(2,1)S(1)} collective-permute-done((bf16[640,640]{1,0:T(8,128)(2,1)}, bf16[640,640]{1,0:T(8,128)(2,1)S(1)}, u32[]{:S(2)}, u32[]{:S(2)}) %collective-permute-start.1) | collective-permute-done | bytes 819232 | tf_op jit(solution)/shard_map/ppermute | solution.py:50
  83.3 0.4 fusion.7
  83.7 7.6 %pad_maximum_fusion = bf16[2560,640]{1,0:T(8,128)(2,1)S(1)} fusion(bf16[640,640]{1,0:T(8,128)(2,1)S(1)} %fusion.11, bf16[640,640]{1,0:T(8,128)(2,1)S(1)} %fusion.7, bf16[640,640]{1,0:T(8,128)(2,1)S(1)} %fusion.3, bf16[640,640]{1,0:T(8,128)(2,1)S(1)} %get-tuple-element.18), kind=kLoop, calls=%fused_computation.7 | loop fusion | flops 13107200 | bytes 6553600 | tf_op jit(solution)/shard_map/concatenate | solution.py:55
  91.3 8.4 %gather_fusion = bf16[2560,640]{1,0:T(8,128)(2,1)} fusion(bf16[2560,640]{1,0:T(8,128)(2,1)S(1)} %pad_maximum_fusion, s32[3072]{0:T(1024)S(1)} %pad_clamp_fusion.1), kind=kCustom, calls=%fused_computation | custom fusion | bytes 6563840 | tf_op jit(solution)/shard_map/gather | solution.py:16
  99.7 7.3 %convolution_convert_fusion.1 = bf16[2560,256]{1,0:T(8,128)(2,1)S(1)} fusion(bf16[2560,2048]{1,0:T(8,128)(2,1)} %all-gather.2.cloned.1.call-done, bf16[640,2048]{1,0:T(8,128)(2,1)} %param.7), kind=kOutput, calls=%fused_computation.6 | convolution fusion | flops 2685009920 | bytes 12845056 | tf_op jit(solution)/shard_map/so,ho->sh/dot_general | solution.py:64
  107.0 0.7 copy-done.6
  107.7 5.9 %convolution_convert_fusion = bf16[2560,384]{1,0:T(8,128)(2,1)S(1)} fusion(bf16[2560,2048]{1,0:T(8,128)(2,1)S(1)} %copy-done.1, bf16[640,2048]{1,0:T(8,128)(2,1)S(1)} %copy-done.6), kind=kOutput, calls=%fused_computation.5 | convolution fusion | flops 4027514880 | bytes 14024704 | tf_op jit(solution)/shard_map/so,ho->sh/dot_general | solution.py:64
  113.6 8.2 %gather_fusion.1 = bf16[2560,256]{1,0:T(8,128)(2,1)} fusion(bf16[2560,256]{1,0:T(8,128)(2,1)S(1)} %convolution_convert_fusion.1, s32[3072]{0:T(1024)S(1)} %pad_clamp_fusion), kind=kCustom, calls=%fused_computation.1 | custom fusion | bytes 2631680 | tf_op jit(solution)/shard_map/gather | solution.py:16
  121.8 2.0 constant_dynamic-slice_fusion.3
  123.7 2.6 %collective-permute-start.3 = (bf16[640,256]{1,0:T(8,128)(2,1)}, bf16[640,256]{1,0:T(8,128)(2,1)}, u32[]{:S(2)}, u32[]{:S(2)}) collective-permute-start(bf16[640,256]{1,0:T(8,128)(2,1)} %get-tuple-element.15), channel_id=1, source_target_pairs={{0,8},{1,9},{2,10},{3,11},{4,12},{5,13},{6,14},{7,15}} | collective-permute-start | bytes 983048 | tf_op jit(solution)/shard_map/ppermute | solution.py:33
  126.3 8.0 %gather_fusion.2 = bf16[2560,384]{1,0:T(8,128)(2,1)} fusion(bf16[2560,384]{1,0:T(8,128)(2,1)S(1)} %convolution_convert_fusion, s32[3072]{0:T(1024)S(1)} %pad_clamp_fusion), kind=kCustom, calls=%fused_computation.2 | custom fusion | bytes 3942400 | tf_op jit(solution)/shard_map/gather | solution.py:16
  134.3 2.4 %constant_dynamic-slice_fusion.1 = (bf16[640,384]{1,0:T(8,128)(2,1)}, bf16[640,384]{1,0:T(8,128)(2,1)}) fusion(bf16[2560,384]{1,0:T(8,128)(2,1)} %gather_fusion.2, s32[]{:T(128)S(6)} %select_n.60, s32[]{:T(128)S(6)} %select_n.63), kind=kLoop, calls=%fused_computation.76 | loop fusion | bytes 1966088 | tf_op jit(solution)/shard_map/dynamic_slice | solution.py:22
  136.7 2.1 collective-permute-start.9
  138.8 1.4 collective-permute-start.6
  140.2 1.5 collective-permute-start.12
  141.6 1.8 add_convert_fusion.7
  143.4 2.0 collective-permute-start.4
  145.4 4.4 %collective-permute-done.9 = bf16[640,384]{1,0:T(8,128)(2,1)} collective-permute-done((bf16[640,384]{1,0:T(8,128)(2,1)}, bf16[640,384]{1,0:T(8,128)(2,1)}, u32[]{:S(2)}, u32[]{:S(2)}) %collective-permute-start.9) | collective-permute-done | bytes 491552 | tf_op jit(solution)/shard_map/ppermute | solution.py:33
  149.9 2.0 add_convert_fusion.3
  151.8 5.2 %collective-permute-start.10 = (bf16[640,384]{1,0:T(8,128)(2,1)}, bf16[640,384]{1,0:T(8,128)(2,1)}, u32[]{:S(2)}, u32[]{:S(2)}) collective-permute-start(bf16[640,384]{1,0:T(8,128)(2,1)} %add_convert_fusion.3), channel_id=1, source_target_pairs={{0,8},{8,16},{1,9},{9,17},{2,10},{10,18},{3,11},{11,19},{4,12},{12... | collective-permute-start | bytes 1474568 | tf_op jit(solution)/shard_map/ppermute | solution.py:33
  157.0 2.1 add_convert_fusion.6
  159.1 0.7 collective-permute-start.7
  159.8 5.4 %collective-permute-done.10 = bf16[640,384]{1,0:T(8,128)(2,1)} collective-permute-done((bf16[640,384]{1,0:T(8,128)(2,1)}, bf16[640,384]{1,0:T(8,128)(2,1)}, u32[]{:S(2)}, u32[]{:S(2)}) %collective-permute-start.10) | collective-permute-done | bytes 491552 | tf_op jit(solution)/shard_map/ppermute | solution.py:33
  165.2 1.4 add_convert_fusion.2
  166.6 0.8 collective-permute-start.13
  167.5 12.1 %fusion.34 = f32[640,2048]{1,0:T(8,128)} fusion(bf16[2560,640]{1,0:T(8,128)(2,1)S(1)} %copy-done.4, bf16[2560,2048]{1,0:T(8,128)(2,1)} %all-gather.2.cloned.1.call-done), kind=kOutput, calls=%fused_computation.79 | convolution fusion | flops 6710886400 | bytes 19005440 | tf_op jit(solution)/shard_map/sh,so->ho/dot_general | solution.py:67
  179.5 6.1 %collective-permute-start.5 = (bf16[640,256]{1,0:T(8,128)(2,1)}, bf16[640,256]{1,0:T(8,128)(2,1)}, u32[]{:S(2)}, u32[]{:S(2)}) collective-permute-start(bf16[640,256]{1,0:T(8,128)(2,1)} %get-tuple-element.13), channel_id=1, source_target_pairs={{0,8},{8,16},{16,24},{1,9},{9,17},{17,25},{2,10},{10,18},{18,26},{... | collective-permute-start | bytes 983048 | tf_op jit(solution)/shard_map/ppermute | solution.py:33
  185.6 0.9 add_convert_fusion.4
  186.5 1.3 collective-permute-start.8
  187.8 5.4 %collective-permute-start.11 = (bf16[640,384]{1,0:T(8,128)(2,1)S(1)}, bf16[640,384]{1,0:T(8,128)(2,1)}, u32[]{:S(2)}, u32[]{:S(2)}) collective-permute-start(bf16[640,384]{1,0:T(8,128)(2,1)S(1)} %get-tuple-element.9), channel_id=1, source_target_pairs={{0,8},{8,16},{16,24},{1,9},{9,17},{17,25},{2,10},{10,18},{18,26},{... | collective-permute-start | bytes 1474568 | tf_op jit(solution)/shard_map/ppermute | solution.py:33
  193.1 0.9 add_convert_fusion
  194.1 1.3 collective-permute-start.14
  195.4 2.2 %convert_reduce_fusion = f32[2048]{0:T(1024)} fusion(bf16[2560,2048]{1,0:T(8,128)(2,1)S(1)} %bitcast.5), kind=kLoop, calls=%fused_computation.4 | loop fusion | flops 10483712 | bytes 10493952 | tf_op jit(solution)/shard_map/reduce_sum | solution.py:68
  197.6 1.2 convert_add_fusion.1
  198.8 1.4 collective-permute-done.11
  200.2 6.1 %collective-permute-done.14 = bf16[640,384]{1,0:T(8,128)(2,1)} collective-permute-done((bf16[640,384]{1,0:T(8,128)(2,1)}, bf16[640,384]{1,0:T(8,128)(2,1)}, u32[]{:S(2)}, u32[]{:S(2)}) %collective-permute-start.14) | collective-permute-done | bytes 491552 | tf_op jit(solution)/shard_map/ppermute | solution.py:34
  206.3 1.3 convert_add_fusion
  207.6 1.3 maximum_multiply_fusion
  (34 shorter events, 0.1 us)
Async XLA Ops:
  7.2 17.6 %copy-start.5 = (bf16[640,640]{1,0:T(8,128)(2,1)S(1)}, bf16[640,640]{1,0:T(8,128)(2,1)}, u32[]{:S(2)}) copy-start(bf16[640,640]{1,0:T(8,128)(2,1)} %param.6) | copy-start | bytes 2457604
  7.2 92.5 %all-gather.2.cloned.1.call-start = ((), (), s32[]{:S(2)}) async-start(), calls=%async_computation | async-start | bytes 11796480 | tf_op jit(solution)/shard_map/all_gather | solution.py:45
  7.9 24.1 %collective-permute-start.2 = (bf16[640,640]{1,0:T(8,128)(2,1)}, bf16[640,640]{1,0:T(8,128)(2,1)S(1)}, u32[]{:S(2)}, u32[]{:S(2)}) collective-permute-start(bf16[640,640]{1,0:T(8,128)(2,1)} %param.6), channel_id=1, source_target_pairs={{0,24},{8,0},{16,8},{24,16},{1,25},{9,1},{17,9},{25,17},{2,26},{10... | collective-permute-start | bytes 2457608 | tf_op jit(solution)/shard_map/ppermute | solution.py:50
  13.0 37.4 %collective-permute-start = (bf16[640,640]{1,0:T(8,128)(2,1)}, bf16[640,640]{1,0:T(8,128)(2,1)S(1)}, u32[]{:S(2)}, u32[]{:S(2)}) collective-permute-start(bf16[640,640]{1,0:T(8,128)(2,1)} %param.6), channel_id=1, source_target_pairs={{0,8},{8,16},{16,24},{24,0},{1,9},{9,17},{17,25},{25,1},{2,10},{10... | collective-permute-start | bytes 2457608 | tf_op jit(solution)/shard_map/ppermute | solution.py:50
  13.0 70.3 %collective-permute-start.1 = (bf16[640,640]{1,0:T(8,128)(2,1)}, bf16[640,640]{1,0:T(8,128)(2,1)S(1)}, u32[]{:S(2)}, u32[]{:S(2)}) collective-permute-start(bf16[640,640]{1,0:T(8,128)(2,1)} %param.6), channel_id=1, source_target_pairs={{0,16},{8,24},{16,0},{24,8},{1,17},{9,25},{17,1},{25,9},{2,18},{10... | collective-permute-start | bytes 2457608 | tf_op jit(solution)/shard_map/ppermute | solution.py:50
  99.7 7.3 %copy-start.1 = (bf16[2560,2048]{1,0:T(8,128)(2,1)S(1)}, bf16[2560,2048]{1,0:T(8,128)(2,1)}, u32[]{:S(2)}) copy-start(bf16[2560,2048]{1,0:T(8,128)(2,1)} %all-gather.2.cloned.1.call-done) | copy-start | bytes 31457284
  99.7 8.0 %copy-start.6 = (bf16[640,2048]{1,0:T(8,128)(2,1)S(1)}, bf16[640,2048]{1,0:T(8,128)(2,1)}, u32[]{:S(2)}) copy-start(bf16[640,2048]{1,0:T(8,128)(2,1)} %param.7) | copy-start | bytes 7864324
  123.7 17.9 %collective-permute-start.3 = (bf16[640,256]{1,0:T(8,128)(2,1)}, bf16[640,256]{1,0:T(8,128)(2,1)}, u32[]{:S(2)}, u32[]{:S(2)}) collective-permute-start(bf16[640,256]{1,0:T(8,128)(2,1)} %get-tuple-element.15), channel_id=1, source_target_pairs={{0,8},{1,9},{2,10},{3,11},{4,12},{5,13},{6,14},{7,15}} | collective-permute-start | bytes 983048 | tf_op jit(solution)/shard_map/ppermute | solution.py:33
  126.3 15.4 %copy-start.2 = (bf16[2560,256]{1,0:T(8,128)(2,1)S(1)}, bf16[2560,256]{1,0:T(8,128)(2,1)}, u32[]{:S(2)}) copy-start(bf16[2560,256]{1,0:T(8,128)(2,1)} %gather_fusion.1) | copy-start | bytes 3932164
  134.3 15.6 %copy-start = (bf16[2560,384]{1,0:T(8,128)(2,1)S(1)}, bf16[2560,384]{1,0:T(8,128)(2,1)}, u32[]{:S(2)}) copy-start(bf16[2560,384]{1,0:T(8,128)(2,1)} %gather_fusion.2) | copy-start | bytes 5898244
  136.7 13.2 %collective-permute-start.9 = (bf16[640,384]{1,0:T(8,128)(2,1)}, bf16[640,384]{1,0:T(8,128)(2,1)}, u32[]{:S(2)}, u32[]{:S(2)}) collective-permute-start(bf16[640,384]{1,0:T(8,128)(2,1)} %get-tuple-element.11), channel_id=1, source_target_pairs={{0,8},{1,9},{2,10},{3,11},{4,12},{5,13},{6,14},{7,15}} | collective-permute-start | bytes 1474568 | tf_op jit(solution)/shard_map/ppermute | solution.py:33
  138.8 18.2 %collective-permute-start.6 = (bf16[640,256]{1,0:T(8,128)(2,1)}, bf16[640,256]{1,0:T(8,128)(2,1)}, u32[]{:S(2)}, u32[]{:S(2)}) collective-permute-start(bf16[640,256]{1,0:T(8,128)(2,1)} %get-tuple-element.16), channel_id=1, source_target_pairs={{24,16},{25,17},{26,18},{27,19},{28,20},{29,21},{30,22},{31,23}} | collective-permute-start | bytes 983048 | tf_op jit(solution)/shard_map/ppermute | solution.py:34
  140.2 19.6 %collective-permute-start.12 = (bf16[640,384]{1,0:T(8,128)(2,1)}, bf16[640,384]{1,0:T(8,128)(2,1)}, u32[]{:S(2)}, u32[]{:S(2)}) collective-permute-start(bf16[640,384]{1,0:T(8,128)(2,1)} %get-tuple-element.12), channel_id=1, source_target_pairs={{24,16},{25,17},{26,18},{27,19},{28,20},{29,21},{30,22},{31,23}} | collective-permute-start | bytes 1474568 | tf_op jit(solution)/shard_map/ppermute | solution.py:34
  143.4 13.6 %collective-permute-start.4 = (bf16[640,256]{1,0:T(8,128)(2,1)}, bf16[640,256]{1,0:T(8,128)(2,1)}, u32[]{:S(2)}, u32[]{:S(2)}) collective-permute-start(bf16[640,256]{1,0:T(8,128)(2,1)} %add_convert_fusion.7), channel_id=1, source_target_pairs={{0,8},{8,16},{1,9},{9,17},{2,10},{10,18},{3,11},{11,19},{4,12},{12... | collective-permute-start | bytes 983048 | tf_op jit(solution)/shard_map/ppermute | solution.py:33
  151.8 13.3 %collective-permute-start.10 = (bf16[640,384]{1,0:T(8,128)(2,1)}, bf16[640,384]{1,0:T(8,128)(2,1)}, u32[]{:S(2)}, u32[]{:S(2)}) collective-permute-start(bf16[640,384]{1,0:T(8,128)(2,1)} %add_convert_fusion.3), channel_id=1, source_target_pairs={{0,8},{8,16},{1,9},{9,17},{2,10},{10,18},{3,11},{11,19},{4,12},{12... | collective-permute-start | bytes 1474568 | tf_op jit(solution)/shard_map/ppermute | solution.py:33
  157.0 10.5 %copy-start.4 = (bf16[2560,640]{1,0:T(8,128)(2,1)S(1)}, bf16[2560,640]{1,0:T(8,128)(2,1)}, u32[]{:S(2)}) copy-start(bf16[2560,640]{1,0:T(8,128)(2,1)} %gather_fusion) | copy-start | bytes 9830404
  159.1 26.5 %collective-permute-start.7 = (bf16[640,256]{1,0:T(8,128)(2,1)S(1)}, bf16[640,256]{1,0:T(8,128)(2,1)S(1)}, u32[]{:S(2)}, u32[]{:S(2)}) collective-permute-start(bf16[640,256]{1,0:T(8,128)(2,1)S(1)} %get-tuple-element.14), channel_id=1, source_target_pairs={{24,16},{16,8},{25,17},{17,9},{26,18},{18,10},{27,19},{19,11},{28,... | collective-permute-start | bytes 983048 | tf_op jit(solution)/shard_map/ppermute | solution.py:34
  166.6 28.8 %slice-start = ((s8[10485760]{0:T(1024)(128)(4,1)}), s8[4194304]{0:T(1024)(128)(4,1)S(1)}, s32[]{:S(2)}) async-start(s8[10485760]{0:T(1024)(128)(4,1)} %bitcast.4), calls=%async_computation.1 | async-start | bytes 8388608
  166.6 28.8 %slice-start.1 = ((s8[10485760]{0:T(1024)(128)(4,1)}), s8[4194304]{0:T(1024)(128)(4,1)S(1)}, s32[]{:S(2)}) async-start(s8[10485760]{0:T(1024)(128)(4,1)} %bitcast.4), calls=%async_computation.2 | async-start | bytes 8388608
  166.6 28.8 %slice-start.2 = ((s8[10485760]{0:T(1024)(128)(4,1)}), s8[2097152]{0:T(1024)(128)(4,1)S(1)}, s32[]{:S(2)}) async-start(s8[10485760]{0:T(1024)(128)(4,1)} %bitcast.4), calls=%async_computation.3 | async-start | bytes 4194304
  166.6 26.5 %collective-permute-start.13 = (bf16[640,384]{1,0:T(8,128)(2,1)S(1)}, bf16[640,384]{1,0:T(8,128)(2,1)S(1)}, u32[]{:S(2)}, u32[]{:S(2)}) collective-permute-start(bf16[640,384]{1,0:T(8,128)(2,1)S(1)} %get-tuple-element.10), channel_id=1, source_target_pairs={{24,16},{16,8},{25,17},{17,9},{26,18},{18,10},{27,19},{19,11},{28,... | collective-permute-start | bytes 1474568 | tf_op jit(solution)/shard_map/ppermute | solution.py:34
  179.5 18.1 %collective-permute-start.5 = (bf16[640,256]{1,0:T(8,128)(2,1)}, bf16[640,256]{1,0:T(8,128)(2,1)}, u32[]{:S(2)}, u32[]{:S(2)}) collective-permute-start(bf16[640,256]{1,0:T(8,128)(2,1)} %get-tuple-element.13), channel_id=1, source_target_pairs={{0,8},{8,16},{16,24},{1,9},{9,17},{17,25},{2,10},{10,18},{18,26},{... | collective-permute-start | bytes 983048 | tf_op jit(solution)/shard_map/ppermute | solution.py:33
  186.5 11.1 %collective-permute-start.8 = (bf16[640,256]{1,0:T(8,128)(2,1)}, bf16[640,256]{1,0:T(8,128)(2,1)}, u32[]{:S(2)}, u32[]{:S(2)}) collective-permute-start(bf16[640,256]{1,0:T(8,128)(2,1)} %add_convert_fusion.4), channel_id=1, source_target_pairs={{24,16},{16,8},{8,0},{25,17},{17,9},{9,1},{26,18},{18,10},{10,2},{... | collective-permute-start | bytes 983048 | tf_op jit(solution)/shard_map/ppermute | solution.py:34
  187.8 12.4 %collective-permute-start.11 = (bf16[640,384]{1,0:T(8,128)(2,1)S(1)}, bf16[640,384]{1,0:T(8,128)(2,1)}, u32[]{:S(2)}, u32[]{:S(2)}) collective-permute-start(bf16[640,384]{1,0:T(8,128)(2,1)S(1)} %get-tuple-element.9), channel_id=1, source_target_pairs={{0,8},{8,16},{16,24},{1,9},{9,17},{17,25},{2,10},{10,18},{18,26},{... | collective-permute-start | bytes 1474568 | tf_op jit(solution)/shard_map/ppermute | solution.py:33
  194.1 12.2 %collective-permute-start.14 = (bf16[640,384]{1,0:T(8,128)(2,1)}, bf16[640,384]{1,0:T(8,128)(2,1)}, u32[]{:S(2)}, u32[]{:S(2)}) collective-permute-start(bf16[640,384]{1,0:T(8,128)(2,1)} %add_convert_fusion), channel_id=1, source_target_pairs={{24,16},{16,8},{8,0},{25,17},{17,9},{9,1},{26,18},{18,10},{10,2},{... | collective-permute-start | bytes 1474568 | tf_op jit(solution)/shard_map/ppermute | solution.py:34
  198.8 8.8 %copy-start.3 = (f32[640,640]{1,0:T(8,128)S(1)}, f32[640,640]{1,0:T(8,128)}, u32[]{:S(2)}) copy-start(f32[640,640]{1,0:T(8,128)} %get-tuple-element.7) | copy-start | bytes 4915204
Sparse Core Ops, SparseCore 0:
  9.9 65.8 all-gather.1

commit v2 on v1

--- a/solution.py
+++ b/solution.py
@@ -1,6 +1,8 @@
 import jax
 import jax.numpy as jnp
 from jax import lax
+from jax.experimental import pallas as pl
+from jax.experimental.pallas import tpu as pltpu
 from jax.sharding import PartitionSpec as P
 
 
@@ -14,6 +16,138 @@
 
 def rows_of(table, index):
     return table.at[index].get(mode="promise_in_bounds", unique_indices=True)
+
+
+def plane_kernel(g_ref, w_ref, full_ref, term_ref, held, weight, send_sem, recv_sem, own_sem, out_sem):
+    t = lax.axis_index("text")
+    core, x, y = t % 2, t // 2 % 2, t // 4
+    across, beside, above = 1 - 2 * core, 2 - 4 * x, 4 - 8 * y
+    mate, xn, yn = t + across, t + beside, t + above
+    diag = t + beside + above
+    rows = g_ref.shape[0]
+    half = rows // 2
+
+    def part(owner, k):
+        return pl.ds(pl.multiple_of(owner * rows + k * half, 16), half)
+
+    barrier = pltpu.get_barrier_semaphore()
+    for other in (mate, xn, yn):
+        pl.semaphore_signal(barrier, inc=1, device_id={"text": other}, device_id_type=pl.DeviceIdType.MESH)
+    pl.semaphore_wait(barrier, 3)
+
+    count = [0]
+
+    def send(src, dst, other):
+        k = count[0]
+        count[0] += 1
+        copy = pltpu.make_async_remote_copy(
+            src_ref=src, dst_ref=held.at[dst], send_sem=send_sem.at[k], recv_sem=recv_sem.at[k],
+            device_id={"text": other}, device_id_type=pl.DeviceIdType.MESH)
+        copy.start()
+        return copy
+
+    outs = []
+
+    def use(owner, k):
+        at = part(owner, k)
+        out = pltpu.make_async_copy(held.at[at], full_ref.at[at], out_sem.at[len(outs)])
+        out.start()
+        outs.append(out)
+        term_ref[at, :] = lax.dot_general(
+            held[at, :], weight[...], (((1,), (1,)), ((), ())),
+            preferred_element_type=jnp.float32).astype(term_ref.dtype)
+
+    def mine(k):
+        return g_ref.at[pl.ds(k * half, half)]
+
+    def pass_on(owner, k, other):
+        return send(held.at[part(owner, k)], part(owner, k), other)
+
+    x0 = send(mine(0), part(t, 0), xn)
+    y0 = send(mine(1), part(t, 1), yn)
+    x1 = send(mine(1), part(t, 1), xn)
+    y1 = send(mine(0), part(t, 0), yn)
+    m0 = send(mine(0), part(t, 0), mate)
+    m1 = send(mine(1), part(t, 1), mate)
+    own = [pltpu.make_async_copy(mine(k), held.at[part(t, k)], own_sem.at[k]) for k in range(2)]
+    load = pltpu.make_async_copy(w_ref, weight, own_sem.at[2])
+    load.start()
+    for copy in own:
+        copy.start()
+    load.wait()
+    for k in range(2):
+        own[k].wait()
+        use(t, k)
+    m0.wait_recv()
+    use(mate, 0)
+    m1.wait_recv()
+    use(mate, 1)
+
+    x0.wait_recv()
+    yf = pass_on(xn, 0, yn)
+    mx0 = pass_on(xn, 0, mate)
+    y0.wait_recv()
+    xf = pass_on(yn, 1, xn)
+    my0 = pass_on(yn, 1, mate)
+    use(xn, 0)
+    use(yn, 1)
+    mx0.wait_recv()
+    use(xn + across, 0)
+    my0.wait_recv()
+    use(yn + across, 1)
+
+    x1.wait_recv()
+    mx1 = pass_on(xn, 1, mate)
+    y1.wait_recv()
+    my1 = pass_on(yn, 0, mate)
+    use(xn, 1)
+    use(yn, 0)
+    mx1.wait_recv()
+    use(xn + across, 1)
+    my1.wait_recv()
+    use(yn + across, 0)
+
+    yf.wait_recv()
+    md0 = pass_on(diag, 0, mate)
+    xf.wait_recv()
+    md1 = pass_on(diag, 1, mate)
+    use(diag, 0)
+    use(diag, 1)
+    md0.wait_recv()
+    use(diag + across, 0)
+    md1.wait_recv()
+    use(diag + across, 1)
+
+    for copy in (x0, y0, x1, y1, m0, m1, yf, mx0, xf, my0, mx1, my1, md0, md1):
+        copy.wait_send()
+    for out in outs:
+        out.wait()
+
+
+def plane_gather(grad_seq, w_out, n_text):
+    rows, columns = grad_seq.shape
+    hidden = w_out.shape[0]
+    slots = rows * n_text
+    anywhere = pl.BlockSpec(memory_space=pl.ANY)
+    return pl.pallas_call(
+        plane_kernel,
+        out_shape=(jax.ShapeDtypeStruct((slots, columns), jnp.bfloat16),
+                   jax.ShapeDtypeStruct((slots, hidden), jnp.bfloat16)),
+        in_specs=[anywhere, anywhere],
+        out_specs=(anywhere, pl.BlockSpec(memory_space=pltpu.VMEM)),
+        scratch_shapes=[
+            pltpu.VMEM((slots, columns), jnp.bfloat16),
+            pltpu.VMEM((hidden, columns), jnp.bfloat16),
+            pltpu.SemaphoreType.DMA((14,)),
+            pltpu.SemaphoreType.DMA((14,)),
+            pltpu.SemaphoreType.DMA((3,)),
+            pltpu.SemaphoreType.DMA((2 * n_text,)),
+        ],
+        compiler_params=pltpu.CompilerParams(
+            collective_id=0, has_side_effects=True, vmem_limit_bytes=40 * 2**20),
+        cost_estimate=pl.CostEstimate(
+            flops=2 * slots * hidden * columns, bytes_accessed=60 * 2**20, transcendentals=0),
+    )(grad_seq, w_out)
 
 
 def line_sum(term, me, n, rows):
@@ -36,18 +170,24 @@
 
 
 def solution(mesh):
-    n_tile = mesh.shape["tile"]
+    n_tile, n_text = mesh.shape["tile"], mesh.shape["text"]
 
     def body(grad_seq, positions, pre_act, w_out):
         local_rows, hidden = pre_act.shape
         slots = positions.shape[0]
         me = lax.axis_index("tile")
-        gathered = lax.all_gather(grad_seq, "text", axis=0, tiled=True)
+        if n_text == 8:
+            gathered, term = plane_gather(grad_seq, w_out, n_text)
+        else:
+            gathered = lax.all_gather(grad_seq, "text", axis=0, tiled=True)
+            term = jnp.einsum(
+                "so,ho->sh", gathered, w_out, preferred_element_type=jnp.float32).astype(jnp.bfloat16)
 
         blocks = [pre_act]
         for shift in range(1, n_tile):
             ring = [(i, (i + shift) % n_tile) for i in range(n_tile)]
             blocks.append(lax.ppermute(pre_act, "tile", ring))
+        blocks = lax.optimization_barrier((blocks, term))[0]
         slot = jnp.arange(slots, dtype=jnp.int32)
         turned = (me - slot // local_rows) % n_tile * local_rows + slot % local_rows
         source = jnp.zeros((slots,), jnp.int32).at[positions].set(
@@ -55,15 +195,12 @@
         act = jnp.concatenate([gelu_parts(b)[0].astype(jnp.bfloat16) for b in blocks], axis=0)
         act_seq = rows_of(act, source)
         slope = gelu_parts(pre_act)[1]
-        gathered, act_seq, slope = lax.optimization_barrier((gathered, act_seq, slope))
 
         cut = hidden // 2 // 128 * 128
         spans = [(0, cut), (cut, hidden)] if cut else [(0, hidden)]
         summed = []
         for lo, hi in spans:
-            term = jnp.einsum("so,ho->sh", gathered, w_out[lo:hi], preferred_element_type=jnp.float32)
-            term = rows_of(term.astype(jnp.bfloat16), positions)
-            summed.append(line_sum(term, me, n_tile, local_rows))
+            summed.append(line_sum(rows_of(term[:, lo:hi], positions), me, n_tile, local_rows))
         weight_term = jnp.einsum("sh,so->ho", act_seq, gathered, preferred_element_type=jnp.float32)
         local_sum = jnp.sum(gathered, axis=0, dtype=jnp.float32)
         grad_pre = jnp.concatenate(summed, axis=1) * slope

time: 216 us -> 179 us (0.83)
  waiting for transfers between devices: 73.8 us -> 8.26 us
  Pallas kernels: 0 us -> 49.6 us
  between operations: 14.3 us -> 0.91 us
  matrix products: 25.3 us -> 12.2 us
  local copies, waits for them, and re-layouts: 39.6 us -> 44.1 us
  starting transfers between devices: 36.4 us -> 32.8 us
  other arithmetic: 26.5 us -> 29.7 us
    ppermute x3, waiting for transfers between devices: 55.8 us -> 0.01 us  [body(): blocks.append(lax.ppermute(pre_act, 'tile', ring))]
    pallas_call x0 -> x1, Pallas kernels: none -> 49.6 us  [plane_gather(): pl.pallas_call(plane_kernel, out_shape=(jax.ShapeDtypeStruct((slots, colu...]
    dot_general x2 -> x0, matrix products: 13.2 us -> none  [body(): jnp.einsum('so,ho->sh', gathered, w_out[lo:hi], preferred_element_type=jn...]
    ppermute x6, waiting for transfers between devices: 6.09 us -> 0.02 us  [line_sum(): lax.ppermute(out_left.astype(jnp.bfloat16), 'tile', [(n - 1 - i, n - 2 -...]
    ppermute x6, starting transfers between devices: 23.3 us -> 18.6 us  [line_sum(): lax.ppermute(out_right.astype(jnp.bfloat16), 'tile', [(i, i + 1) for i in...]
    reduce_sum x1, other arithmetic: 2.23 us -> 6.29 us  [body(): local_sum = jnp.sum(gathered, axis=0, dtype=jnp.float32)]
    ppermute x6, waiting for transfers between devices: 11.2 us -> 8.23 us  [line_sum(): lax.ppermute(out_right.astype(jnp.bfloat16), 'tile', [(i, i + 1) for i in...]
    convert_element_type x4, other arithmetic: 7.29 us -> 4.49 us  [line_sum(): out_right.astype(jnp.bfloat16)]
  transfers between devices with their start and end apart: 16 -> 15, of which waited for: 7 -> 2; matrix products, arithmetic and copies ran while one was open for 30% -> 45% of each run, Pallas kernels for 0% -> 28%
where the time goes in v2:
time: 179 us; the launch traced here: 178 us
  Pallas kernels  49.6 us (28%)
  local copies, waits for them, and re-layouts  44.1 us (25%)
  starting transfers between devices  32.8 us (18%)
  other arithmetic  29.7 us (17%)
  matrix products  12.2 us (7%)
  waiting for transfers between devices  8.26 us (5%)
    pallas_call x1, Pallas kernels, plane_gather(): pl.pallas_call(plane_kernel, out_shape=(jax.ShapeDtypeStruct((slots, colu...  49.6 us
    gather x3, local copies, waits for them, and re-layouts, rows_of(): return table.at[index].get(mode='promise_in_bounds', unique_indices=True)  25.4 us
    ppermute x6, starting transfers between devices, line_sum(): lax.ppermute(out_right.astype(jnp.bfloat16), 'tile', [(i, i + 1) for i in...  18.6 us
    dot_general x1, matrix products, body(): jnp.einsum('sh,so->ho', act_seq, gathered, preferred_element_type=jnp.flo...  12.2 us
    scatter x1, local copies, waits for them, and re-layouts, body(): jnp.zeros((slots,), jnp.int32).at[positions]  9.92 us
    ppermute x6, waiting for transfers between devices, line_sum(): lax.ppermute(out_right.astype(jnp.bfloat16), 'tile', [(i, i + 1) for i in...  8.23 us
    concatenate x1, other arithmetic, body(): jnp.concatenate([gelu_parts(b)[0].astype(jnp.bfloat16) for b in blocks],...  7.52 us
    ppermute x6, starting transfers between devices, line_sum(): lax.ppermute(out_left.astype(jnp.bfloat16), 'tile', [(n - 1 - i, n - 2 -...  7.12 us
  transfers between devices with their start and end apart: 15, of which 2 were waited for; matrix products, arithmetic and copies ran while one was open for 45% of the time, Pallas kernels for 28%

profile of v2, /device:TPU:0, one launch (start us, length us, event | category | flops | bytes accessed | tf_op | source)
XLA Modules:
  0.0 177.6 jit_solution(2249930816652468103)
XLA Ops:
  0.6 3.1 %collective-permute-start.12 = (bf16[640,640]{1,0:T(8,128)(2,1)}, bf16[640,640]{1,0:T(8,128)(2,1)}, u32[]{:S(2)}, u32[]{:S(2)}) collective-permute-start(bf16[640,640]{1,0:T(8,128)(2,1)} %param.6), channel_id=1, source_target_pairs={{0,8},{8,16},{16,24},{24,0},{1,9},{9,17},{17,25},{25,1},{2,10},{10... | collective-permute-start | bytes 2457608 | tf_op jit(solution)/shard_map/ppermute | solution.py:189
  3.7 2.6 %collective-permute-start.13 = (bf16[640,640]{1,0:T(8,128)(2,1)}, bf16[640,640]{1,0:T(8,128)(2,1)}, u32[]{:S(2)}, u32[]{:S(2)}) collective-permute-start(bf16[640,640]{1,0:T(8,128)(2,1)} %param.6), channel_id=1, source_target_pairs={{0,16},{8,24},{16,0},{24,8},{1,17},{9,25},{17,1},{25,9},{2,18},{10... | collective-permute-start | bytes 2457608 | tf_op jit(solution)/shard_map/ppermute | solution.py:189
  6.3 1.3 collective-permute-start.14
  7.7 0.7 compare_select_fusion.1
  8.4 0.0 copy-start
  8.4 1.7 copy-done
  10.2 1.3 copy-done.1
  11.5 49.6 %shard_map.67 = (bf16[2560,2048]{1,0:T(8,128)(2,1)}, bf16[2560,640]{1,0:T(8,128)(2,1)S(1)}) custom-call(bf16[320,2048]{1,0:T(8,128)(2,1)S(1)} %copy-done.1, bf16[640,2048]{1,0:T(8,128)(2,1)S(1)} %copy-done), custom_call_target="tpu_custom_call" | custom-call | flops 6710886400 | bytes 62914560 | tf_op jit(solution)/shard_map/pallas_call | solution.py:132
  61.1 1.1 slice.6
  62.3 8.3 %gather_fusion = bf16[2560,256]{1,0:T(8,128)(2,1)} fusion(bf16[2560,256]{1,0:T(8,128)(2,1)} %slice.6, s32[3072]{0:T(1024)S(1)} %pad_clamp_fusion.1), kind=kCustom, calls=%fused_computation | custom fusion | bytes 2631680 | tf_op jit(solution)/shard_map/gather | solution.py:18
  70.5 1.9 %constant_dynamic-slice_fusion.3 = (bf16[640,256]{1,0:T(8,128)(2,1)}, bf16[640,256]{1,0:T(8,128)(2,1)}) fusion(bf16[2560,256]{1,0:T(8,128)(2,1)} %gather_fusion, s32[]{:T(128)S(6)} %select_n.56, s32[]{:T(128)S(6)} %select_n.59), kind=kLoop, calls=%fused_computation.78 | loop fusion | bytes 1310728 | tf_op jit(solution)/shard_map/dynamic_slice | solution.py:156
  72.5 3.3 %collective-permute-start = (bf16[640,256]{1,0:T(8,128)(2,1)}, bf16[640,256]{1,0:T(8,128)(2,1)}, u32[]{:S(2)}, u32[]{:S(2)}) collective-permute-start(bf16[640,256]{1,0:T(8,128)(2,1)} %get-tuple-element.21), channel_id=1, source_target_pairs={{0,8},{1,9},{2,10},{3,11},{4,12},{5,13},{6,14},{7,15}} | collective-permute-start | bytes 983048 | tf_op jit(solution)/shard_map/ppermute | solution.py:167
  75.8 1.5 slice.7
  77.3 8.7 %gather_fusion.1 = bf16[2560,384]{1,0:T(8,128)(2,1)S(1)} fusion(bf16[2560,384]{1,0:T(8,128)(2,1)} %slice.7, s32[3072]{0:T(1024)S(1)} %pad_clamp_fusion.1), kind=kCustom, calls=%fused_computation.1 | custom fusion | bytes 3942400 | tf_op jit(solution)/shard_map/gather | solution.py:18
  85.9 1.2 constant_dynamic-slice_fusion.1
  87.1 2.1 %collective-permute-start.6 = (bf16[640,384]{1,0:T(8,128)(2,1)}, bf16[640,384]{1,0:T(8,128)(2,1)}, u32[]{:S(2)}, u32[]{:S(2)}) collective-permute-start(bf16[640,384]{1,0:T(8,128)(2,1)} %get-tuple-element.17), channel_id=1, source_target_pairs={{0,8},{1,9},{2,10},{3,11},{4,12},{5,13},{6,14},{7,15}} | collective-permute-start | bytes 1474568 | tf_op jit(solution)/shard_map/ppermute | solution.py:167
  89.2 6.3 %convert_reduce_fusion = f32[2048]{0:T(1024)} fusion(bf16[2560,2048]{1,0:T(8,128)(2,1)} %get-tuple-element.14), kind=kLoop, calls=%fused_computation.4 | loop fusion | flops 10483712 | bytes 10493952 | tf_op jit(solution)/shard_map/reduce_sum | solution.py:205
  95.5 9.9 %scatter_custom_fusion = s32[2560]{0:T(1024)S(1)} fusion(s32[2560]{0:T(1024)S(1)} %get-tuple-element.27, s32[2560]{0:T(1024)S(1)} %get-tuple-element.28, s32[]{:T(128)} %constant.46.clone.1), kind=kCustom, calls=%fused_computation.73 | custom fusion | bytes 10244 | tf_op jit(solution)/shard_map/scatter | solution.py:193
  105.4 0.0 copy-start.6
  105.5 0.8 collective-permute-start.3
  106.3 1.1 add_convert_fusion.7
  107.4 0.0 collective-permute-done.6
  107.4 1.3 collective-permute-start.1
  108.7 0.0 copy-start.4
  108.7 1.2 add_convert_fusion.3
  110.0 0.7 collective-permute-start.9
  110.7 5.4 %collective-permute-done.1 = bf16[640,256]{1,0:T(8,128)(2,1)S(1)} collective-permute-done((bf16[640,256]{1,0:T(8,128)(2,1)S(1)}, bf16[640,256]{1,0:T(8,128)(2,1)S(1)}, u32[]{:S(2)}, u32[]{:S(2)}) %collective-permute-start.1) | collective-permute-done | bytes 327712 | tf_op jit(solution)/shard_map/ppermute | solution.py:167
  116.1 4.4 %collective-permute-start.7 = (bf16[640,384]{1,0:T(8,128)(2,1)S(1)}, bf16[640,384]{1,0:T(8,128)(2,1)S(1)}, u32[]{:S(2)}, u32[]{:S(2)}) collective-permute-start(bf16[640,384]{1,0:T(8,128)(2,1)S(1)} %add_convert_fusion.3), channel_id=1, source_target_pairs={{0,8},{8,16},{1,9},{9,17},{2,10},{10,18},{3,11},{11,19},{4,12},{12... | collective-permute-start | bytes 1474568 | tf_op jit(solution)/shard_map/ppermute | solution.py:167
  120.5 1.0 add_convert_fusion.6
  121.5 1.4 collective-permute-start.4
  122.9 2.5 %collective-permute-start.2 = (bf16[640,256]{1,0:T(8,128)(2,1)}, bf16[640,256]{1,0:T(8,128)(2,1)}, u32[]{:S(2)}, u32[]{:S(2)}) collective-permute-start(bf16[640,256]{1,0:T(8,128)(2,1)} %get-tuple-element.19), channel_id=1, source_target_pairs={{0,8},{8,16},{16,24},{1,9},{9,17},{17,25},{2,10},{10,18},{18,26},{... | collective-permute-start | bytes 983048 | tf_op jit(solution)/shard_map/ppermute | solution.py:167
  125.5 1.8 %fusion.3 = (bf16[640,640]{1,0:T(8,128)(2,1)S(1)}, bf16[640,640]{1,0:T(8,128)(2,1)S(1)}) fusion(bf16[640,640]{1,0:T(8,128)(2,1)S(1)} %copy-done.4, bf16[640,640]{1,0:T(8,128)(2,1)} %collective-permute-done.12), kind=kLoop, calls=%fused_computation.21 | loop fusion | flops 4915200 | bytes 3276800 | tf_op jit(solution)/shard_map/convert_element_type | solution.py:195
  127.3 1.9 %fusion.11 = (bf16[640,640]{1,0:T(8,128)(2,1)S(1)}, bf16[640,640]{1,0:T(8,128)(2,1)S(1)}) fusion(bf16[640,640]{1,0:T(8,128)(2,1)} %collective-permute-done.13, bf16[640,640]{1,0:T(8,128)(2,1)} %collective-permute-done.14), kind=kLoop, calls=%fused_computation.29 | loop fusion | flops 4915200 | bytes 3276800 | tf_op jit(solution)/shard_map/convert_element_type | solution.py:195
  129.3 2.8 %collective-permute-done.7 = bf16[640,384]{1,0:T(8,128)(2,1)S(1)} collective-permute-done((bf16[640,384]{1,0:T(8,128)(2,1)S(1)}, bf16[640,384]{1,0:T(8,128)(2,1)S(1)}, u32[]{:S(2)}, u32[]{:S(2)}) %collective-permute-start.7) | collective-permute-done | bytes 491552 | tf_op jit(solution)/shard_map/ppermute | solution.py:167
  132.1 1.2 add_convert_fusion.2
  133.3 1.4 collective-permute-start.10
  134.7 7.5 %pad_maximum_fusion = bf16[2560,640]{1,0:T(8,128)(2,1)S(1)} fusion(bf16[640,640]{1,0:T(8,128)(2,1)S(1)} %get-tuple-element.26, bf16[640,640]{1,0:T(8,128)(2,1)S(1)} %get-tuple-element.25, bf16[640,640]{1,0:T(8,128)(2,1)S(1)} %get-tuple-element.24, bf16[640,640]{1,0:T(8,128)(2,1)S(1)} %get-tuple-element.23), kind=kLoop, calls=%fused_computation.5 | loop fusion | flops 13107200 | bytes 6553600 | tf_op jit(solution)/shard_map/concatenate | solution.py:195
  142.2 8.4 %gather_fusion.2 = bf16[2560,640]{1,0:T(8,128)(2,1)} fusion(bf16[2560,640]{1,0:T(8,128)(2,1)S(1)} %pad_maximum_fusion, s32[3072]{0:T(1024)S(1)} %pad_clamp_fusion), kind=kCustom, calls=%fused_computation.2 | custom fusion | bytes 6563840 | tf_op jit(solution)/shard_map/gather | solution.py:18
  150.7 1.2 add_convert_fusion.4
  151.8 1.3 collective-permute-start.5
  153.1 4.9 %collective-permute-start.8 = (bf16[640,384]{1,0:T(8,128)(2,1)}, bf16[640,384]{1,0:T(8,128)(2,1)S(1)}, u32[]{:S(2)}, u32[]{:S(2)}) collective-permute-start(bf16[640,384]{1,0:T(8,128)(2,1)} %get-tuple-element.15), channel_id=1, source_target_pairs={{0,8},{8,16},{16,24},{1,9},{9,17},{17,25},{2,10},{10,18},{18,26},{... | collective-permute-start | bytes 1474568 | tf_op jit(solution)/shard_map/ppermute | solution.py:167
  158.1 1.3 add_convert_fusion
  159.4 1.5 collective-permute-start.11
  160.9 12.2 %fusion.36 = f32[640,2048]{1,0:T(8,128)} fusion(bf16[2560,640]{1,0:T(8,128)(2,1)} %gather_fusion.2, bf16[2560,2048]{1,0:T(8,128)(2,1)} %get-tuple-element.14), kind=kOutput, calls=%fused_computation.79 | convolution fusion | flops 6710886400 | bytes 19005440 | tf_op jit(solution)/shard_map/sh,so->ho/dot_general | solution.py:204
  173.1 1.2 convert_add_fusion.1
  174.4 0.0 copy-start.5
  174.4 1.3 convert_add_fusion
  175.7 1.9 %fusion.20 = f32[640,640]{1,0:T(8,128)} fusion(bf16[640,640]{1,0:T(8,128)(2,1)S(1)} %copy-done.5, f32[640,384]{1,0:T(8,128)S(1)} %convert_add_fusion, f32[640,256]{1,0:T(8,128)S(1)} %convert_add_fusion.1), kind=kLoop, calls=%fused_computation.38 | loop fusion | flops 4505600 | bytes 4096000 | tf_op jit(solution)/shard_map/mul | solution.py:206
  (23 shorter events, 0.1 us)
Async XLA Ops:
  0.6 120.9 %collective-permute-start.12 = (bf16[640,640]{1,0:T(8,128)(2,1)}, bf16[640,640]{1,0:T(8,128)(2,1)}, u32[]{:S(2)}, u32[]{:S(2)}) collective-permute-start(bf16[640,640]{1,0:T(8,128)(2,1)} %param.6), channel_id=1, source_target_pairs={{0,8},{8,16},{16,24},{24,0},{1,9},{9,17},{17,25},{25,1},{2,10},{10... | collective-permute-start | bytes 2457608 | tf_op jit(solution)/shard_map/ppermute | solution.py:189
  3.7 119.2 %collective-permute-start.13 = (bf16[640,640]{1,0:T(8,128)(2,1)}, bf16[640,640]{1,0:T(8,128)(2,1)}, u32[]{:S(2)}, u32[]{:S(2)}) collective-permute-start(bf16[640,640]{1,0:T(8,128)(2,1)} %param.6), channel_id=1, source_target_pairs={{0,16},{8,24},{16,0},{24,8},{1,17},{9,25},{17,1},{25,9},{2,18},{10... | collective-permute-start | bytes 2457608 | tf_op jit(solution)/shard_map/ppermute | solution.py:189
  6.3 119.1 %collective-permute-start.14 = (bf16[640,640]{1,0:T(8,128)(2,1)}, bf16[640,640]{1,0:T(8,128)(2,1)}, u32[]{:S(2)}, u32[]{:S(2)}) collective-permute-start(bf16[640,640]{1,0:T(8,128)(2,1)} %param.6), channel_id=1, source_target_pairs={{0,24},{8,0},{16,8},{24,16},{1,25},{9,1},{17,9},{25,17},{2,26},{10... | collective-permute-start | bytes 2457608 | tf_op jit(solution)/shard_map/ppermute | solution.py:189
  8.4 1.7 copy-start
  10.2 1.3 copy-start.1
  72.5 33.0 %collective-permute-start = (bf16[640,256]{1,0:T(8,128)(2,1)}, bf16[640,256]{1,0:T(8,128)(2,1)}, u32[]{:S(2)}, u32[]{:S(2)}) collective-permute-start(bf16[640,256]{1,0:T(8,128)(2,1)} %get-tuple-element.21), channel_id=1, source_target_pairs={{0,8},{1,9},{2,10},{3,11},{4,12},{5,13},{6,14},{7,15}} | collective-permute-start | bytes 983048 | tf_op jit(solution)/shard_map/ppermute | solution.py:167
  85.9 46.1 %copy-start.2 = (bf16[2560,384]{1,0:T(8,128)(2,1)}, bf16[2560,384]{1,0:T(8,128)(2,1)S(1)}, u32[]{:S(2)}) copy-start(bf16[2560,384]{1,0:T(8,128)(2,1)S(1)} %gather_fusion.1) | copy-start | bytes 5898244
  87.1 20.3 %collective-permute-start.6 = (bf16[640,384]{1,0:T(8,128)(2,1)}, bf16[640,384]{1,0:T(8,128)(2,1)}, u32[]{:S(2)}, u32[]{:S(2)}) collective-permute-start(bf16[640,384]{1,0:T(8,128)(2,1)} %get-tuple-element.17), channel_id=1, source_target_pairs={{0,8},{1,9},{2,10},{3,11},{4,12},{5,13},{6,14},{7,15}} | collective-permute-start | bytes 1474568 | tf_op jit(solution)/shard_map/ppermute | solution.py:167
  89.2 17.1 %copy-start.3 = (bf16[2560,256]{1,0:T(8,128)(2,1)S(1)}, bf16[2560,256]{1,0:T(8,128)(2,1)}, u32[]{:S(2)}) copy-start(bf16[2560,256]{1,0:T(8,128)(2,1)} %gather_fusion) | copy-start | bytes 3932164
  105.4 4.5 %copy-start.6 = (bf16[640,384]{1,0:T(8,128)(2,1)S(1)}, bf16[640,384]{1,0:T(8,128)(2,1)}, u32[]{:S(2)}) copy-start(bf16[640,384]{1,0:T(8,128)(2,1)} %get-tuple-element.18) | copy-start | bytes 1474564
  105.5 4.5 %collective-permute-start.3 = (bf16[640,256]{1,0:T(8,128)(2,1)}, bf16[640,256]{1,0:T(8,128)(2,1)S(1)}, u32[]{:S(2)}, u32[]{:S(2)}) collective-permute-start(bf16[640,256]{1,0:T(8,128)(2,1)} %get-tuple-element.22), channel_id=1, source_target_pairs={{24,16},{25,17},{26,18},{27,19},{28,20},{29,21},{30,22},{31,23}} | collective-permute-start | bytes 983048 | tf_op jit(solution)/shard_map/ppermute | solution.py:168
  107.4 8.7 %collective-permute-start.1 = (bf16[640,256]{1,0:T(8,128)(2,1)S(1)}, bf16[640,256]{1,0:T(8,128)(2,1)S(1)}, u32[]{:S(2)}, u32[]{:S(2)}) collective-permute-start(bf16[640,256]{1,0:T(8,128)(2,1)S(1)} %add_convert_fusion.7), channel_id=1, source_target_pairs={{0,8},{8,16},{1,9},{9,17},{2,10},{10,18},{3,11},{11,19},{4,12},{12... | collective-permute-start | bytes 983048 | tf_op jit(solution)/shard_map/ppermute | solution.py:167
  108.7 16.7 %copy-start.4 = (bf16[640,640]{1,0:T(8,128)(2,1)S(1)}, bf16[640,640]{1,0:T(8,128)(2,1)}, u32[]{:S(2)}) copy-start(bf16[640,640]{1,0:T(8,128)(2,1)} %param.6) | copy-start | bytes 2457604
  110.0 19.3 %collective-permute-start.9 = (bf16[640,384]{1,0:T(8,128)(2,1)S(1)}, bf16[640,384]{1,0:T(8,128)(2,1)S(1)}, u32[]{:S(2)}, u32[]{:S(2)}) collective-permute-start(bf16[640,384]{1,0:T(8,128)(2,1)S(1)} %copy-done.6), channel_id=1, source_target_pairs={{24,16},{25,17},{26,18},{27,19},{28,20},{29,21},{30,22},{31,23}} | collective-permute-start | bytes 1474568 | tf_op jit(solution)/shard_map/ppermute | solution.py:168
  116.1 16.0 %collective-permute-start.7 = (bf16[640,384]{1,0:T(8,128)(2,1)S(1)}, bf16[640,384]{1,0:T(8,128)(2,1)S(1)}, u32[]{:S(2)}, u32[]{:S(2)}) collective-permute-start(bf16[640,384]{1,0:T(8,128)(2,1)S(1)} %add_convert_fusion.3), channel_id=1, source_target_pairs={{0,8},{8,16},{1,9},{9,17},{2,10},{10,18},{3,11},{11,19},{4,12},{12... | collective-permute-start | bytes 1474568 | tf_op jit(solution)/shard_map/ppermute | solution.py:167
  121.5 29.1 %collective-permute-start.4 = (bf16[640,256]{1,0:T(8,128)(2,1)}, bf16[640,256]{1,0:T(8,128)(2,1)}, u32[]{:S(2)}, u32[]{:S(2)}) collective-permute-start(bf16[640,256]{1,0:T(8,128)(2,1)} %get-tuple-element.20), channel_id=1, source_target_pairs={{24,16},{16,8},{25,17},{17,9},{26,18},{18,10},{27,19},{19,11},{28,... | collective-permute-start | bytes 983048 | tf_op jit(solution)/shard_map/ppermute | solution.py:168
  122.9 50.2 %collective-permute-start.2 = (bf16[640,256]{1,0:T(8,128)(2,1)}, bf16[640,256]{1,0:T(8,128)(2,1)}, u32[]{:S(2)}, u32[]{:S(2)}) collective-permute-start(bf16[640,256]{1,0:T(8,128)(2,1)} %get-tuple-element.19), channel_id=1, source_target_pairs={{0,8},{8,16},{16,24},{1,9},{9,17},{17,25},{2,10},{10,18},{18,26},{... | collective-permute-start | bytes 983048 | tf_op jit(solution)/shard_map/ppermute | solution.py:167
  133.3 24.8 %collective-permute-start.10 = (bf16[640,384]{1,0:T(8,128)(2,1)}, bf16[640,384]{1,0:T(8,128)(2,1)}, u32[]{:S(2)}, u32[]{:S(2)}) collective-permute-start(bf16[640,384]{1,0:T(8,128)(2,1)} %get-tuple-element.16), channel_id=1, source_target_pairs={{24,16},{16,8},{25,17},{17,9},{26,18},{18,10},{27,19},{19,11},{28,... | collective-permute-start | bytes 1474568 | tf_op jit(solution)/shard_map/ppermute | solution.py:168
  151.8 21.3 %collective-permute-start.5 = (bf16[640,256]{1,0:T(8,128)(2,1)S(1)}, bf16[640,256]{1,0:T(8,128)(2,1)S(1)}, u32[]{:S(2)}, u32[]{:S(2)}) collective-permute-start(bf16[640,256]{1,0:T(8,128)(2,1)S(1)} %add_convert_fusion.4), channel_id=1, source_target_pairs={{24,16},{16,8},{8,0},{25,17},{17,9},{9,1},{26,18},{18,10},{10,2},{... | collective-permute-start | bytes 983048 | tf_op jit(solution)/shard_map/ppermute | solution.py:168
  153.1 21.2 %collective-permute-start.8 = (bf16[640,384]{1,0:T(8,128)(2,1)}, bf16[640,384]{1,0:T(8,128)(2,1)S(1)}, u32[]{:S(2)}, u32[]{:S(2)}) collective-permute-start(bf16[640,384]{1,0:T(8,128)(2,1)} %get-tuple-element.15), channel_id=1, source_target_pairs={{0,8},{8,16},{16,24},{1,9},{9,17},{17,25},{2,10},{10,18},{18,26},{... | collective-permute-start | bytes 1474568 | tf_op jit(solution)/shard_map/ppermute | solution.py:167
  159.4 15.0 %collective-permute-start.11 = (bf16[640,384]{1,0:T(8,128)(2,1)S(1)}, bf16[640,384]{1,0:T(8,128)(2,1)S(1)}, u32[]{:S(2)}, u32[]{:S(2)}) collective-permute-start(bf16[640,384]{1,0:T(8,128)(2,1)S(1)} %add_convert_fusion), channel_id=1, source_target_pairs={{24,16},{16,8},{8,0},{25,17},{17,9},{9,1},{26,18},{18,10},{10,2},{... | collective-permute-start | bytes 1474568 | tf_op jit(solution)/shard_map/ppermute | solution.py:168
  174.4 1.4 copy-start.5

commit v3 on v2

--- a/solution.py
+++ b/solution.py
@@ -150,6 +150,172 @@
     )(grad_seq, w_out)
 
 
+def line_kernel(n, subs, width, term_ref, pre_refs, place_ref, full_ref, grad_ref, weight_ref, bias_ref,
+                act, turned, full, out, arrive, leave, send_sem, recv_sem, load_sem, out_sem):
+    me = lax.axis_index("tile")
+    rows, hidden = pre_refs[0].shape
+    slots, columns = full_ref.shape
+    size = rows // subs
+    mesh_ids = pl.DeviceIdType.MESH
+    barrier = pltpu.get_barrier_semaphore()
+
+    for other in ((me + 1) % n, (me + n - 1) % n):
+        pl.semaphore_signal(barrier, inc=1, device_id={"tile": other}, device_id_type=mesh_ids)
+    pl.semaphore_wait(barrier, 2)
+
+    load = pltpu.make_async_copy(full_ref, full, load_sem)
+    load.start()
+
+    def hop(way, step, j, src):
+        k = ((way * (n - 1)) + step - 1) * subs + j
+        return pltpu.make_async_remote_copy(
+            src_ref=src, dst_ref=arrive.at[way, step - 1, pl.ds(j * size, size)],
+            send_sem=send_sem.at[k], recv_sem=recv_sem.at[k],
+            device_id={"tile": me + 1 - 2 * way}, device_id_type=mesh_ids)
+
+    def place(way):
+        return me if way == 0 else n - 1 - me
+
+    def poll(step, j):
+        piece = pl.ds(j * size, size)
+        for way in range(2):
+            i = place(way)
+
+            def own():
+                block = me + n - step if way == 0 else me - n + step
+                return pl.ds(pl.multiple_of(block * rows + j * size, 16), size)
+
+            @pl.when(i == 0)
+            def _():
+                hop(way, step, j, term_ref.at[own()]).start()
+
+            if step > 1:
+                @pl.when((i >= 1) & (i <= step - 1))
+                def _():
+                    hop(way, step - 1, j, leave.at[way, step - 2, piece]).wait_recv()
+                    total = (term_ref[own(), :].astype(jnp.float32)
+                             + arrive[way, step - 2, piece, :].astype(jnp.float32))
+                    leave[way, step - 1, piece, :] = total.astype(jnp.bfloat16)
+                    hop(way, step, j, leave.at[way, step - 1, piece]).start()
+
+    def last(j):
+        piece = pl.ds(j * size, size)
+        for way in range(2):
+            @pl.when(place(way) >= 1)
+            def _():
+                hop(way, n - 1, j, leave.at[way, n - 2, piece]).wait_recv()
+        own = pl.ds(pl.multiple_of(me * rows + j * size, 16), size)
+        chunk = 32
+        inside_right, inside_left = me > 0, me < n - 1
+
+        def finish(c, carry):
+            at = pl.ds(pl.multiple_of(j * size + c * chunk, 16), chunk)
+            total = term_ref[pl.ds(pl.multiple_of(me * rows + j * size + c * chunk, 16), chunk), :].astype(jnp.float32)
+            right = arrive[0, n - 2, at, :].astype(jnp.float32)
+            left = arrive[1, n - 2, at, :].astype(jnp.float32)
+            total = total + jnp.where(inside_right, right, 0.0) + jnp.where(inside_left, left, 0.0)
+            grad_ref[at, :] = total * gelu_parts(pre_refs[0][at, :])[1]
+            return carry
+
+        lax.fori_loop(0, size // chunk, finish, 0)
+
+    def activate(k):
+        chunk = 32
+
+        def run(c, carry):
+            at = pl.ds(pl.multiple_of(c * chunk, chunk), chunk)
+            to = pl.ds(pl.multiple_of(k * rows + c * chunk, chunk), chunk)
+            act[to, :] = gelu_parts(pre_refs[k][at, :])[0].astype(jnp.bfloat16)
+            return carry
+
+        lax.fori_loop(0, rows // chunk, run, 0)
+
+    def reorder(first, count):
+        def run(c, carry):
+            start = pl.multiple_of(c * width, width)
+            row = lax.broadcasted_iota(jnp.int32, (width, slots), 0) + start
+            chosen = jnp.where(row == place_ref[...], 1.0, 0.0).astype(jnp.bfloat16)
+            moved = lax.dot_general(chosen, act[...], (((1,), (0,)), ((), ())), preferred_element_type=jnp.float32)
+            turned[:, pl.ds(start, width)] = moved.T.astype(jnp.bfloat16)
+            return carry
+
+        lax.fori_loop(first, first + count, run, 0)
+
+    def weigh(first, count):
+        def run(c, carry):
+            at = pl.ds(pl.multiple_of(c * width, width), width)
+            out[:, at] = jnp.dot(turned[...], full[:, at], preferred_element_type=jnp.float32)
+            ones = jnp.ones((16, slots), jnp.bfloat16)
+            bias_ref[:, at] = jnp.dot(ones, full[:, at], preferred_element_type=jnp.float32)[:1]
+            return carry
+
+        lax.fori_loop(first, first + count, run, 0)
+
+    work = [lambda k=k: activate(k) for k in range(n)]
+    work += [lambda c=c: reorder(c, 1) for c in range(slots // width)]
+    work.append(load.wait)
+    work += [lambda c=c: weigh(c, 1) for c in range(columns // width)]
+
+    for j in range(subs):
+        poll(1, j)
+    gaps = (n - 1) * subs
+    done = 0
+    for g in range(gaps):
+        upto = len(work) * (g + 1) // gaps
+        for item in work[done:upto]:
+            item()
+        done = upto
+        step, j = g // subs + 2, g % subs
+        if g == gaps - 1:
+            flush = pltpu.make_async_copy(out, weight_ref, out_sem)
+            flush.start()
+        if step < n:
+            poll(step, j)
+        else:
+            last(j)
+    flush.wait()
+    for way in range(2):
+        for step in range(1, n):
+            @pl.when(place(way) <= step - 1)
+            def _():
+                for j in range(subs):
+                    hop(way, step, j, leave.at[way, step - 1, pl.ds(j * size, size)]).wait_send()
+
+
+def line_finish(n, term, blocks, places, gathered):
+    rows, hidden = blocks[0].shape
+    slots, columns = gathered.shape
+    subs, width = 4, 256
+    anywhere, vmem = pl.BlockSpec(memory_space=pl.ANY), pl.BlockSpec(memory_space=pltpu.VMEM)
+
+    def kernel(*refs):
+        line_kernel(n, subs, width, refs[0], refs[1:n + 1], *refs[n + 1:])
+
+    count = 2 * (n - 1) * subs
+    return pl.pallas_call(
+        kernel,
+        out_shape=(jax.ShapeDtypeStruct((rows, hidden), jnp.float32),
+                   jax.ShapeDtypeStruct((hidden, columns), jnp.float32),
+                   jax.ShapeDtypeStruct((1, columns), jnp.float32)),
+        in_specs=[vmem] * (n + 2) + [anywhere],
+        out_specs=(vmem, anywhere, vmem),
+        scratch_shapes=[
+            pltpu.VMEM((slots, hidden), jnp.bfloat16),
+            pltpu.VMEM((hidden, slots), jnp.bfloat16),
+            pltpu.VMEM((slots, columns), jnp.bfloat16),
+            pltpu.VMEM((hidden, columns), jnp.float32),
+            pltpu.VMEM((2, n - 1, rows, hidden), jnp.bfloat16),
+            pltpu.VMEM((2, n - 1, rows, hidden), jnp.bfloat16),
+            pltpu.SemaphoreType.DMA((count,)),
+            pltpu.SemaphoreType.DMA((count,)),
+            pltpu.SemaphoreType.DMA,
+            pltpu.SemaphoreType.DMA,
+        ],
+        compiler_params=pltpu.CompilerParams(
+            collective_id=1, has_side_effects=True, vmem_limit_bytes=60 * 2**20),
+    )(term, *blocks, places, gathered)
+
+
 def line_sum(term, me, n, rows):
     def mine(block):
         start = jnp.clip(block, 0, n - 1) * rows
@@ -187,6 +353,13 @@
         for shift in range(1, n_tile):
             ring = [(i, (i + shift) % n_tile) for i in range(n_tile)]
             blocks.append(lax.ppermute(pre_act, "tile", ring))
+        if n_text == 8:
+            tiles = [(me - k) % n_tile for k in range(n_tile)]
+            places = jnp.concatenate([
+                lax.dynamic_slice_in_dim(positions, t * local_rows, local_rows) for t in tiles]).reshape(1, slots)
+            grad_pre, weight_term, bias = line_finish(
+                n_tile, rows_of(term, positions), blocks, places, gathered)
+            return (grad_pre, weight_term, bias.reshape(-1))
         blocks = lax.optimization_barrier((blocks, term))[0]
         slot = jnp.arange(slots, dtype=jnp.int32)
         turned = (me - slot // local_rows) % n_tile * local_rows + slot % local_rows

time: 179 us -> 145 us (0.81)
  Pallas kernels: 49.6 us -> 112 us
  other arithmetic: 29.7 us -> 0.72 us
  starting transfers between devices: 32.8 us -> 7.95 us
  local copies, waits for them, and re-layouts: 44.1 us -> 21.8 us
  matrix products: 12.2 us -> 0 us
  waiting for transfers between devices: 8.26 us -> 0.01 us
    pallas_call x0 -> x1, Pallas kernels: none -> 62 us  [line_finish(): pl.pallas_call(kernel, out_shape=(jax.ShapeDtypeStruct((rows, hidden), jn...]
    ppermute x12 -> x0, starting transfers between devices: 25.7 us -> none  [the longest x6 18.6 us: line_sum(): lax.ppermute(out_right.astype(jnp.bfloat16), 'tile', [(i, i + 1) for i in...]
    gather x3 -> x1, local copies, waits for them, and re-layouts: 25.4 us -> 8.42 us  [rows_of(): return table.at[index].get(mode='promise_in_bounds', unique_indices=True)]
    dot_general x1 -> x0, matrix products: 12.2 us -> none  [body(): jnp.einsum('sh,so->ho', act_seq, gathered, preferred_element_type=jnp.flo...]
    convert_element_type x8 -> x0, other arithmetic: 10.7 us -> none  [the longest x4 4.49 us: line_sum(): out_right.astype(jnp.bfloat16)]
    scatter x1 -> x0, local copies, waits for them, and re-layouts: 9.92 us -> none  [body(): jnp.zeros((slots,), jnp.int32).at[positions]]
    unnamed x14 -> x9, local copies, waits for them, and re-layouts: 3.08 us -> 11.9 us
    ppermute x12 -> x0, waiting for transfers between devices: 8.25 us -> none  [the longest x6 8.23 us: line_sum(): lax.ppermute(out_right.astype(jnp.bfloat16), 'tile', [(i, i + 1) for i in...]
  transfers between devices with their start and end apart: 15 -> 3, of which waited for: 2 -> 0; matrix products, arithmetic and copies ran while one was open for 45% -> 7% of each run, Pallas kernels for 28% -> 35%
where the time goes in v3:
time: 145 us; the launch traced here: 143 us
  Pallas kernels  112 us (77%)
  local copies, waits for them, and re-layouts  21.8 us (15%)
  starting transfers between devices  7.95 us (5%)
    pallas_call x1, Pallas kernels, line_finish(): pl.pallas_call(kernel, out_shape=(jax.ShapeDtypeStruct((rows, hidden), jn...  62 us
    pallas_call x1, Pallas kernels, plane_gather(): pl.pallas_call(plane_kernel, out_shape=(jax.ShapeDtypeStruct((slots, colu...  49.6 us
    unnamed x9, local copies, waits for them, and re-layouts  11.9 us
    gather x1, local copies, waits for them, and re-layouts, rows_of(): return table.at[index].get(mode='promise_in_bounds', unique_indices=True)  8.42 us
    ppermute x3, starting transfers between devices, body(): blocks.append(lax.ppermute(pre_act, 'tile', ring))  7.95 us
  transfers between devices with their start and end apart: 3, of which 0 were waited for; matrix products, arithmetic and copies ran while one was open for 7% of the time, Pallas kernels for 35%

profile of v3, /device:TPU:0, one launch (start us, length us, event | category | flops | bytes accessed | tf_op | source)
XLA Modules:
  0.0 142.8 jit_solution(504315882873931475)
XLA Ops:
  0.6 4.1 %collective-permute-start.1 = (bf16[640,640]{1,0:T(8,128)(2,1)}, bf16[640,640]{1,0:T(8,128)(2,1)}, u32[]{:S(2)}, u32[]{:S(2)}) collective-permute-start(bf16[640,640]{1,0:T(8,128)(2,1)} %refs_1_.1), channel_id=1, source_target_pairs={{0,16},{8,24},{16,0},{24,8},{1,17},{9,25},{17,1},{25,9},{2,18},{10... | collective-permute-start | bytes 2457608 | tf_op jit(solution)/shard_map/ppermute | solution.py:355
  4.8 1.6 %collective-permute-start = (bf16[640,640]{1,0:T(8,128)(2,1)}, bf16[640,640]{1,0:T(8,128)(2,1)}, u32[]{:S(2)}, u32[]{:S(2)}) collective-permute-start(bf16[640,640]{1,0:T(8,128)(2,1)} %refs_1_.1), channel_id=1, source_target_pairs={{0,8},{8,16},{16,24},{24,0},{1,9},{9,17},{17,25},{25,1},{2,10},{10... | collective-permute-start | bytes 2457608 | tf_op jit(solution)/shard_map/ppermute | solution.py:355
  6.3 2.2 %collective-permute-start.2 = (bf16[640,640]{1,0:T(8,128)(2,1)}, bf16[640,640]{1,0:T(8,128)(2,1)}, u32[]{:S(2)}, u32[]{:S(2)}) collective-permute-start(bf16[640,640]{1,0:T(8,128)(2,1)} %refs_1_.1), channel_id=1, source_target_pairs={{0,24},{8,0},{16,8},{24,16},{1,25},{9,1},{17,9},{25,17},{2,26},{10... | collective-permute-start | bytes 2457608 | tf_op jit(solution)/shard_map/ppermute | solution.py:355
  8.6 0.7 compare_select_fusion
  9.3 0.9 fusion
  10.2 0.6 reshape.12.refs_5_
  10.8 0.0 copy-start
  10.8 1.7 %copy-done = bf16[640,2048]{1,0:T(8,128)(2,1)S(1)} copy-done((bf16[640,2048]{1,0:T(8,128)(2,1)S(1)}, bf16[640,2048]{1,0:T(8,128)(2,1)}, u32[]{:S(2)}) %copy-start) | copy-done | bytes 2621464
  12.6 0.0 copy-start.1
  12.6 1.3 copy-done.1
  13.9 49.6 %shard_map.67 = (bf16[2560,2048]{1,0:T(8,128)(2,1)}, bf16[2560,640]{1,0:T(8,128)(2,1)S(1)}) custom-call(bf16[320,2048]{1,0:T(8,128)(2,1)S(1)} %copy-done.1, bf16[640,2048]{1,0:T(8,128)(2,1)S(1)} %copy-done), custom_call_target="tpu_custom_call" | custom-call | flops 6710886400 | bytes 62914560 | tf_op jit(solution)/shard_map/pallas_call | solution.py:132
  63.5 8.4 %gather_fusion = bf16[2560,640]{1,0:T(8,128)(2,1)} fusion(bf16[2560,640]{1,0:T(8,128)(2,1)S(1)} %get-tuple-element.8, s32[3072]{0:T(1024)S(1)} %pad_clamp_fusion), kind=kCustom, calls=%fused_computation | custom fusion | bytes 6563840 | tf_op jit(solution)/shard_map/gather | solution.py:18
  72.0 0.0 collective-permute-done.1.refs_3_
  72.0 0.0 collective-permute-done.refs_2_
  72.0 0.0 collective-permute-done.2.refs_4_
  72.0 62.0 %shard_map.68 = (f32[640,640]{1,0:T(8,128)}, f32[640,2048]{1,0:T(8,128)}, f32[1,2048]{1,0:T(1,128)}) custom-call(bf16[2560,640]{1,0:T(8,128)(2,1)} %gather_fusion, bf16[640,640]{1,0:T(8,128)(2,1)} %refs_1_.1, bf16[640,640]{1,0:T(8,128)(2,1)} %collective-permute-done.refs_2_, bf16[640,640]{1,0:T(8,128)(2,1)} %collective-permute-done.1.refs_3_, ...), custom_call_target="tpu_custom_call" | custom-call | tf_op jit(solution)/shard_map/pallas_call | solution.py:295
  134.0 2.7 %copy.10 = f32[640,640]{1,0:T(8,128)} copy(f32[640,640]{1,0:T(8,128)} %get-tuple-element.20) | data formatting | bytes 3276800
  136.7 0.0 copy-start.2
  136.7 5.5 %copy.11 = f32[640,2048]{1,0:T(8,128)} copy(f32[640,2048]{1,0:T(8,128)} %get-tuple-element.21) | data formatting | bytes 10485760
  142.2 0.0 copy-done.2
  142.2 0.6 copy.12
  (2 shorter events, 0.0 us)
Async XLA Ops:
  0.6 71.3 %collective-permute-start.1 = (bf16[640,640]{1,0:T(8,128)(2,1)}, bf16[640,640]{1,0:T(8,128)(2,1)}, u32[]{:S(2)}, u32[]{:S(2)}) collective-permute-start(bf16[640,640]{1,0:T(8,128)(2,1)} %refs_1_.1), channel_id=1, source_target_pairs={{0,16},{8,24},{16,0},{24,8},{1,17},{9,25},{17,1},{25,9},{2,18},{10... | collective-permute-start | bytes 2457608 | tf_op jit(solution)/shard_map/ppermute | solution.py:355
  4.8 67.2 %collective-permute-start = (bf16[640,640]{1,0:T(8,128)(2,1)}, bf16[640,640]{1,0:T(8,128)(2,1)}, u32[]{:S(2)}, u32[]{:S(2)}) collective-permute-start(bf16[640,640]{1,0:T(8,128)(2,1)} %refs_1_.1), channel_id=1, source_target_pairs={{0,8},{8,16},{16,24},{24,0},{1,9},{9,17},{17,25},{25,1},{2,10},{10... | collective-permute-start | bytes 2457608 | tf_op jit(solution)/shard_map/ppermute | solution.py:355
  6.3 65.6 %collective-permute-start.2 = (bf16[640,640]{1,0:T(8,128)(2,1)}, bf16[640,640]{1,0:T(8,128)(2,1)}, u32[]{:S(2)}, u32[]{:S(2)}) collective-permute-start(bf16[640,640]{1,0:T(8,128)(2,1)} %refs_1_.1), channel_id=1, source_target_pairs={{0,24},{8,0},{16,8},{24,16},{1,25},{9,1},{17,9},{25,17},{2,26},{10... | collective-permute-start | bytes 2457608 | tf_op jit(solution)/shard_map/ppermute | solution.py:355
  10.8 1.7 %copy-start = (bf16[640,2048]{1,0:T(8,128)(2,1)S(1)}, bf16[640,2048]{1,0:T(8,128)(2,1)}, u32[]{:S(2)}) copy-start(bf16[640,2048]{1,0:T(8,128)(2,1)} %w_ref.1) | copy-start | bytes 7864324
  12.6 1.3 copy-start.1
  136.7 5.5 %copy-start.2 = (f32[1,2048]{1,0:T(1,128)S(1)}, f32[1,2048]{1,0:T(1,128)}, u32[]{:S(2)}) copy-start(f32[1,2048]{1,0:T(1,128)} %get-tuple-element.12) | copy-start | bytes 24580

commit v4 on v3

--- a/solution.py
+++ b/solution.py
@@ -144,14 +144,14 @@
             pltpu.SemaphoreType.DMA((2 * n_text,)),
         ],
         compiler_params=pltpu.CompilerParams(
-            collective_id=0, has_side_effects=True, vmem_limit_bytes=40 * 2**20),
+            collective_id=0, has_side_effects=True, vmem_limit_bytes=60 * 2**20),
         cost_estimate=pl.CostEstimate(
             flops=2 * slots * hidden * columns, bytes_accessed=60 * 2**20, transcendentals=0),
     )(grad_seq, w_out)
 
 
 def line_kernel(n, subs, width, term_ref, pre_refs, place_ref, full_ref, grad_ref, weight_ref, bias_ref,
-                act, turned, full, out, arrive, leave, send_sem, recv_sem, load_sem, out_sem):
+                act, turned, full, arrive, leave, send_sem, recv_sem, load_sem):
     me = lax.axis_index("tile")
     rows, hidden = pre_refs[0].shape
     slots, columns = full_ref.shape
@@ -244,7 +244,7 @@
     def weigh(first, count):
         def run(c, carry):
             at = pl.ds(pl.multiple_of(c * width, width), width)
-            out[:, at] = jnp.dot(turned[...], full[:, at], preferred_element_type=jnp.float32)
+            weight_ref[:, at] = jnp.dot(turned[...], full[:, at], preferred_element_type=jnp.float32)
             ones = jnp.ones((16, slots), jnp.bfloat16)
             bias_ref[:, at] = jnp.dot(ones, full[:, at], preferred_element_type=jnp.float32)[:1]
             return carry
@@ -266,14 +266,10 @@
             item()
         done = upto
         step, j = g // subs + 2, g % subs
-        if g == gaps - 1:
-            flush = pltpu.make_async_copy(out, weight_ref, out_sem)
-            flush.start()
         if step < n:
             poll(step, j)
         else:
             last(j)
-    flush.wait()
     for way in range(2):
         for step in range(1, n):
             @pl.when(place(way) <= step - 1)
@@ -298,21 +294,19 @@
                    jax.ShapeDtypeStruct((hidden, columns), jnp.float32),
                    jax.ShapeDtypeStruct((1, columns), jnp.float32)),
         in_specs=[vmem] * (n + 2) + [anywhere],
-        out_specs=(vmem, anywhere, vmem),
+        out_specs=(vmem, vmem, vmem),
         scratch_shapes=[
             pltpu.VMEM((slots, hidden), jnp.bfloat16),
             pltpu.VMEM((hidden, slots), jnp.bfloat16),
             pltpu.VMEM((slots, columns), jnp.bfloat16),
-            pltpu.VMEM((hidden, columns), jnp.float32),
             pltpu.VMEM((2, n - 1, rows, hidden), jnp.bfloat16),
             pltpu.VMEM((2, n - 1, rows, hidden), jnp.bfloat16),
             pltpu.SemaphoreType.DMA((count,)),
             pltpu.SemaphoreType.DMA((count,)),
             pltpu.SemaphoreType.DMA,
-            pltpu.SemaphoreType.DMA,
         ],
         compiler_params=pltpu.CompilerParams(
-            collective_id=1, has_side_effects=True, vmem_limit_bytes=60 * 2**20),
+            collective_id=1, has_side_effects=True, vmem_limit_bytes=40 * 2**20),
     )(term, *blocks, places, gathered)
 
 

time: 145 us -> 138 us (0.952)
  local copies, waits for them, and re-layouts: 21.8 us -> 17 us
  Pallas kernels: 112 us -> 110 us
    unnamed x9 -> x5, local copies, waits for them, and re-layouts: 11.9 us -> 5.26 us
    pallas_call x1, Pallas kernels: 62 us -> 58.8 us  [line_finish(): pl.pallas_call(kernel, out_shape=(jax.ShapeDtypeStruct((rows, hidden), jn...]
    gather x1, local copies, waits for them, and re-layouts: 8.42 us -> 10.8 us  [rows_of(): return table.at[index].get(mode='promise_in_bounds', unique_indices=True)]
    pallas_call x1, Pallas kernels: 49.6 us -> 51.7 us  [plane_gather(): pl.pallas_call(plane_kernel, out_shape=(jax.ShapeDtypeStruct((slots, colu...]
  transfers between devices with their start and end apart: 3 -> 3, of which waited for: 0 -> 0; matrix products, arithmetic and copies ran while one was open for 7% -> 9% of each run, Pallas kernels for 35% -> 38%
where the time goes in v4:
time: 138 us; the launch traced here: 137 us
  Pallas kernels  110 us (80%)
  local copies, waits for them, and re-layouts  17 us (12%)
  starting transfers between devices  7.95 us (6%)
    pallas_call x1, Pallas kernels, line_finish(): pl.pallas_call(kernel, out_shape=(jax.ShapeDtypeStruct((rows, hidden), jn...  58.8 us
    pallas_call x1, Pallas kernels, plane_gather(): pl.pallas_call(plane_kernel, out_shape=(jax.ShapeDtypeStruct((slots, colu...  51.7 us
    gather x1, local copies, waits for them, and re-layouts, rows_of(): return table.at[index].get(mode='promise_in_bounds', unique_indices=True)  10.8 us
    ppermute x3, starting transfers between devices, body(): blocks.append(lax.ppermute(pre_act, 'tile', ring))  7.95 us
    unnamed x5, local copies, waits for them, and re-layouts  5.26 us
  transfers between devices with their start and end apart: 3, of which 0 were waited for; matrix products, arithmetic and copies ran while one was open for 9% of the time, Pallas kernels for 38%

profile of v4, /device:TPU:0, one launch (start us, length us, event | category | flops | bytes accessed | tf_op | source)
XLA Modules:
  0.0 136.9 jit_solution(9936916216409355634)
XLA Ops:
  0.6 4.1 %collective-permute-start.1 = (bf16[640,640]{1,0:T(8,128)(2,1)}, bf16[640,640]{1,0:T(8,128)(2,1)}, u32[]{:S(2)}, u32[]{:S(2)}) collective-permute-start(bf16[640,640]{1,0:T(8,128)(2,1)} %refs_1_.1), channel_id=1, source_target_pairs={{0,16},{8,24},{16,0},{24,8},{1,17},{9,25},{17,1},{25,9},{2,18},{10... | collective-permute-start | bytes 2457608 | tf_op jit(solution)/shard_map/ppermute | solution.py:349
  4.8 1.6 %collective-permute-start = (bf16[640,640]{1,0:T(8,128)(2,1)}, bf16[640,640]{1,0:T(8,128)(2,1)}, u32[]{:S(2)}, u32[]{:S(2)}) collective-permute-start(bf16[640,640]{1,0:T(8,128)(2,1)} %refs_1_.1), channel_id=1, source_target_pairs={{0,8},{8,16},{16,24},{24,0},{1,9},{9,17},{17,25},{25,1},{2,10},{10... | collective-permute-start | bytes 2457608 | tf_op jit(solution)/shard_map/ppermute | solution.py:349
  6.3 2.2 %collective-permute-start.2 = (bf16[640,640]{1,0:T(8,128)(2,1)}, bf16[640,640]{1,0:T(8,128)(2,1)}, u32[]{:S(2)}, u32[]{:S(2)}) collective-permute-start(bf16[640,640]{1,0:T(8,128)(2,1)} %refs_1_.1), channel_id=1, source_target_pairs={{0,24},{8,0},{16,8},{24,16},{1,25},{9,1},{17,9},{25,17},{2,26},{10... | collective-permute-start | bytes 2457608 | tf_op jit(solution)/shard_map/ppermute | solution.py:349
  8.6 0.7 compare_select_fusion
  9.3 0.9 fusion
  10.3 51.7 %shard_map.67 = (bf16[2560,2048]{1,0:T(8,128)(2,1)}, bf16[2560,640]{1,0:T(8,128)(2,1)}) custom-call(bf16[320,2048]{1,0:T(8,128)(2,1)} %g_ref.1, bf16[640,2048]{1,0:T(8,128)(2,1)} %w_ref.1), custom_call_target="tpu_custom_call" | custom-call | flops 6710886400 | bytes 62914560 | tf_op jit(solution)/shard_map/pallas_call | solution.py:132
  62.0 10.8 %gather_fusion = bf16[2560,640]{1,0:T(8,128)(2,1)S(1)} fusion(bf16[2560,640]{1,0:T(8,128)(2,1)} %get-tuple-element.8, s32[3072]{0:T(1024)S(1)} %pad_clamp_fusion), kind=kCustom, calls=%fused_computation | custom fusion | bytes 6563840 | tf_op jit(solution)/shard_map/gather | solution.py:18
  72.8 0.0 collective-permute-done.1.refs_3_
  72.8 0.0 collective-permute-done.refs_2_
  72.8 0.0 collective-permute-done.2.refs_4_
  72.8 0.0 copy-start
  72.8 1.1 copy-done
  74.0 58.8 %shard_map.68 = (f32[640,640]{1,0:T(8,128)S(1)}, f32[640,2048]{1,0:T(8,128)S(1)}, f32[1,2048]{1,0:T(1,128)S(1)}) custom-call(bf16[2560,640]{1,0:T(8,128)(2,1)S(1)} %gather_fusion, bf16[640,640]{1,0:T(8,128)(2,1)S(1)} %copy-done, bf16[640,640]{1,0:T(8,128)(2,1)} %collective-permute-done.refs_2_, bf16[640,640]{1,0:T(8,128)(2,1)} %collective-permute-done.1.refs_3_, ...), custom_call_target="tpu_custom_call" | custom-call | tf_op jit(solution)/shard_map/pallas_call | solution.py:291
  132.7 1.2 copy.10
  133.9 2.4 %copy.11 = f32[640,2048]{1,0:T(8,128)} copy(f32[640,2048]{1,0:T(8,128)S(1)} %get-tuple-element.21) | data formatting | bytes 10485760
  136.3 0.6 copy.12
  (3 shorter events, 0.0 us)
Async XLA Ops:
  0.6 72.2 %collective-permute-start.1 = (bf16[640,640]{1,0:T(8,128)(2,1)}, bf16[640,640]{1,0:T(8,128)(2,1)}, u32[]{:S(2)}, u32[]{:S(2)}) collective-permute-start(bf16[640,640]{1,0:T(8,128)(2,1)} %refs_1_.1), channel_id=1, source_target_pairs={{0,16},{8,24},{16,0},{24,8},{1,17},{9,25},{17,1},{25,9},{2,18},{10... | collective-permute-start | bytes 2457608 | tf_op jit(solution)/shard_map/ppermute | solution.py:349
  4.8 68.1 %collective-permute-start = (bf16[640,640]{1,0:T(8,128)(2,1)}, bf16[640,640]{1,0:T(8,128)(2,1)}, u32[]{:S(2)}, u32[]{:S(2)}) collective-permute-start(bf16[640,640]{1,0:T(8,128)(2,1)} %refs_1_.1), channel_id=1, source_target_pairs={{0,8},{8,16},{16,24},{24,0},{1,9},{9,17},{17,25},{25,1},{2,10},{10... | collective-permute-start | bytes 2457608 | tf_op jit(solution)/shard_map/ppermute | solution.py:349
  6.3 66.5 %collective-permute-start.2 = (bf16[640,640]{1,0:T(8,128)(2,1)}, bf16[640,640]{1,0:T(8,128)(2,1)}, u32[]{:S(2)}, u32[]{:S(2)}) collective-permute-start(bf16[640,640]{1,0:T(8,128)(2,1)} %refs_1_.1), channel_id=1, source_target_pairs={{0,24},{8,0},{16,8},{24,16},{1,25},{9,1},{17,9},{25,17},{2,26},{10... | collective-permute-start | bytes 2457608 | tf_op jit(solution)/shard_map/ppermute | solution.py:349
  72.8 1.1 copy-start
